TPU v7x, 512 devices: a whole 4x4x16 slice. The times are simulated.
512 devices in a mesh: group: 16 (over z), shard: 32 (over y, x, core).
Axes of the slice: x: 4, y: 4, z: 16, core: 2. Of those that a mesh axis runs over, the one named last changes fastest.
Arguments:
- entry_grads: float32 [16, 32, 256, 1280], P('group', 'shard'), may hold values from -800 to 800
- exit_grads: float32 [16, 32, 256, 1024], P('group', 'shard'), may hold values from -800 to 800
- entry_params: float32 [32, 256, 1280], P('shard', 'group'), may hold values from -0.15625 to 0.15625
- exit_params: float32 [32, 256, 1024], P('shard', 'group'), may hold values from -0.15625 to 0.15625
- entry_mean: float32 [32, 256, 1280], P('shard', 'group'), may hold values from -1.5 to 1.5
- exit_mean: float32 [32, 256, 1024], P('shard', 'group'), may hold values from -1.5 to 1.5
- entry_square: float32 [32, 256, 1280], P('shard', 'group'), may hold values from 0.01 to 1
- exit_square: float32 [32, 256, 1024], P('shard', 'group'), may hold values from 0.01 to 1
Outputs:
- entry_master: float32 [32, 256, 1280], P('shard', 'group')
- exit_master: float32 [32, 256, 1024], P('shard', 'group')
- entry_moment: float32 [32, 256, 1280], P('shard', 'group')
- exit_moment: float32 [32, 256, 1024], P('shard', 'group')
- entry_variance: float32 [32, 256, 1280], P('shard', 'group')
- exit_variance: float32 [32, 256, 1024], P('shard', 'group')
- entry_weights: bfloat16 [32, 256, 1280], P('shard')
- exit_weights: bfloat16 [32, 256, 1024], P('shard')
All inputs are finite; a program needn't handle non-finite values.
Results may differ from a plain program's by a relative error of at most 0.0004.
Values may be sent and summed in bfloat16 or wider, within the bound.
No kernel may reach another device: no remote copies, remote signals or barrier semaphores. Data moves between devices by JAX's collectives and lax.ppermute only.
A program may use at most 64 MiB of HBM per device.

v0:
```python
import jax
import jax.numpy as jnp
from jax import lax
from jax.sharding import PartitionSpec as P

beta_first = 0.9
beta_second = 0.95
learn_rate = 0.01
decay_rate = 0.1
epsilon = 1e-08
correct_first = 1.0 - 0.9**40
correct_second = 1.0 - 0.95**40


def adamw_step(params, mean, square, total, clip):
    grads = clip * total
    moment = beta_first * mean + (1.0 - beta_first) * grads
    variance = beta_second * square + (1.0 - beta_second) * grads * grads
    update = moment / correct_first / (jnp.sqrt(variance / correct_second) + epsilon)
    master = params - learn_rate * (update + decay_rate * params)
    return (master, moment, variance)


def body(
    entry_grads,
    exit_grads,
    entry_params,
    exit_params,
    entry_mean,
    exit_mean,
    entry_square,
    exit_square,
):
    entry_rows_dev = entry_grads.shape[2]
    exit_rows_dev = exit_grads.shape[2]
    entry_width = entry_grads.shape[3]
    exit_width = exit_grads.shape[3]
    entry_local = entry_grads.reshape(entry_rows_dev, entry_width)
    exit_local = exit_grads.reshape(exit_rows_dev, exit_width)
    entry_total, exit_total = (
        lax.psum_scatter(entry_local, "group", scatter_dimension=0, tiled=True),
        lax.psum_scatter(exit_local, "group", scatter_dimension=0, tiled=True),
    )
    partial_value = jnp.sum(entry_total * entry_total) + jnp.sum(exit_total * exit_total)
    squares = lax.psum(partial_value, ("group", "shard"))
    count = (entry_rows_dev * entry_width + exit_rows_dev * exit_width) * lax.axis_size("shard")
    limit = jnp.sqrt(jnp.float32(count))
    clip = jnp.minimum(jnp.float32(1.0), limit / (jnp.sqrt(squares) + 1e-06))
    entry_master, entry_moment, entry_variance = adamw_step(
        entry_params[0], entry_mean[0], entry_square[0], entry_total, clip
    )
    exit_master, exit_moment, exit_variance = adamw_step(
        exit_params[0], exit_mean[0], exit_square[0], exit_total, clip
    )
    entry_round = entry_master.astype(jnp.bfloat16)
    exit_round = exit_master.astype(jnp.bfloat16)
    entry_weights = lax.all_gather(entry_round, "group", axis=0, tiled=True)
    exit_weights = lax.all_gather(exit_round, "group", axis=0, tiled=True)
    return (
        entry_master[None],
        exit_master[None],
        entry_moment[None],
        exit_moment[None],
        entry_variance[None],
        exit_variance[None],
        entry_weights[None],
        exit_weights[None],
    )


def solution(mesh):
    placed = (
        P("group", "shard", None, None),
        P("group", "shard", None, None),
        P("shard", "group", None),
        P("shard", "group", None),
        P("shard", "group", None),
        P("shard", "group", None),
        P("shard", "group", None),
        P("shard", "group", None),
    )
    return jax.shard_map(
        body,
        mesh=mesh,
        in_specs=placed,
        out_specs=(
            P("shard", "group", None),
            P("shard", "group", None),
            P("shard", "group", None),
            P("shard", "group", None),
            P("shard", "group", None),
            P("shard", "group", None),
            P("shard", None, None),
            P("shard", None, None),
        ),
        check_vma=False,
    )
```

profile of v0, /device:TPU:6, one launch (start us, length us, event | category | flops | bytes accessed | tf_op | source)
XLA Modules:
  0.0 335.2 jit_solution(14248556409421145714)
XLA Ops:
  7.2 0.0 copy-start.1
  7.2 0.0 reduce-scatter.5.cloned.1.call-start
  7.2 0.7 reduce-scatter.5.cloned.1.call-update
  7.9 0.0 reduce-scatter.3.cloned.1.call-start
  8.0 0.0 copy-start.4
  8.0 0.0 copy-start.5
  8.0 0.0 copy-start.6
  8.0 0.7 reduce-scatter.3.cloned.1.call-update
  8.7 77.0 %reduce-scatter.5.cloned.1.call-done = f32[16,1024]{1,0:T(8,128)} async-done(((f32[256,1024]{1,0:T(8,128)}), f32[16,1024]{1,0:T(8,128)}) %reduce-scatter.5.cloned.1.call-update) | async-done | bytes 65552 | tf_op jit(solution)/shard_map/reduce_scatter | solution.py:42
  85.7 1.5 multiply_reduce_fusion.1
  87.2 70.3 %reduce-scatter.3.cloned.1.call-done = f32[16,1280]{1,0:T(8,128)} async-done(((f32[256,1280]{1,0:T(8,128)}), f32[16,1280]{1,0:T(8,128)}) %reduce-scatter.3.cloned.1.call-update) | async-done | bytes 81936 | tf_op jit(solution)/shard_map/reduce_scatter | solution.py:41
  157.5 1.5 multiply_reduce_fusion
  160.4 100.9 %psum.7 = f32[]{:T(128)} all-reduce(f32[]{:T(128)S(6)} %add.42), channel_id=1, replica_groups=mesh['group'=16,'shard'=32] {'group','shard'}, use_global_device_ids=true, to_apply=%region_4.0 | all-reduce | flops 1 | bytes 8 | tf_op jit(solution)/shard_map/psum | solution.py:45
  262.0 0.0 copy-done.1
  262.0 0.0 copy-done.2
  262.1 0.0 copy-done.3
  262.1 1.6 fusion.11
  263.7 31.3 %all_gather.6 = bf16[256,1280]{1,0:T(8,128)(2,1)S(1)} all-gather(bf16[16,1280]{1,0:T(8,128)(2,1)S(1)} %get-tuple-element.10), channel_id=1, replica_groups=mesh['group'=16,'shard'=32] {'group'}, dimensions={0}, use_global_device_ids=true | all-gather | bytes 696320 | tf_op jit(solution)/shard_map/all_gather | solution.py:57
  295.0 0.0 copy-done.6
  295.0 0.0 copy-done
  295.0 0.7 fusion.10
  295.7 31.0 %all_gather.7 = bf16[256,1024]{1,0:T(8,128)(2,1)S(1)} all-gather(bf16[16,1024]{1,0:T(8,128)(2,1)S(1)} %get-tuple-element.8), channel_id=1, replica_groups=mesh['group'=16,'shard'=32] {'group'}, dimensions={0}, use_global_device_ids=true | all-gather | bytes 557056 | tf_op jit(solution)/shard_map/all_gather | solution.py:58
  326.7 0.8 copy.18
  327.5 0.8 copy.19
  (5 shorter events, 0.0 us)
Async XLA Ops:
  7.2 254.9 %copy-start.1 = (f32[1,16,1280]{2,1,0:T(8,128)S(1)}, f32[1,16,1280]{2,1,0:T(8,128)}, u32[]{:S(2)}) copy-start(f32[1,16,1280]{2,1,0:T(8,128)} %param.14) | copy-start | bytes 245764
  7.2 254.9 %copy-start.2 = (f32[1,16,1280]{2,1,0:T(8,128)S(1)}, f32[1,16,1280]{2,1,0:T(8,128)}, u32[]{:S(2)}) copy-start(f32[1,16,1280]{2,1,0:T(8,128)} %param.12) | copy-start | bytes 245764
  7.2 254.9 %copy-start.3 = (f32[1,16,1280]{2,1,0:T(8,128)S(1)}, f32[1,16,1280]{2,1,0:T(8,128)}, u32[]{:S(2)}) copy-start(f32[1,16,1280]{2,1,0:T(8,128)} %param.10) | copy-start | bytes 245764
  7.2 78.5 %reduce-scatter.5.cloned.1.call-start = ((), (), s32[]{:S(2)}) async-start(), calls=%async_computation.3 | async-start | bytes 1114112 | tf_op jit(solution)/shard_map/reduce_scatter | solution.py:42
  7.9 149.6 %reduce-scatter.3.cloned.1.call-start = ((), (), s32[]{:S(2)}) async-start(), calls=%async_computation.2 | async-start | bytes 1392640 | tf_op jit(solution)/shard_map/reduce_scatter | solution.py:41
  8.0 287.0 %copy-start.4 = (f32[1,16,1024]{2,1,0:T(8,128)S(1)}, f32[1,16,1024]{2,1,0:T(8,128)}, u32[]{:S(2)}) copy-start(f32[1,16,1024]{2,1,0:T(8,128)} %param.15) | copy-start | bytes 196612
  8.0 287.0 %copy-start.5 = (f32[1,16,1024]{2,1,0:T(8,128)S(1)}, f32[1,16,1024]{2,1,0:T(8,128)}, u32[]{:S(2)}) copy-start(f32[1,16,1024]{2,1,0:T(8,128)} %param.13) | copy-start | bytes 196612
  8.0 287.0 %copy-start.6 = (f32[1,16,1024]{2,1,0:T(8,128)S(1)}, f32[1,16,1024]{2,1,0:T(8,128)}, u32[]{:S(2)}) copy-start(f32[1,16,1024]{2,1,0:T(8,128)} %param.11) | copy-start | bytes 196612
  85.7 209.3 %copy-start = (f32[16,1024]{1,0:T(8,128)S(1)}, f32[16,1024]{1,0:T(8,128)}, u32[]{:S(2)}) copy-start(f32[16,1024]{1,0:T(8,128)} %reduce-scatter.5.cloned.1.call-done) | copy-start | bytes 196612
Sparse Core Ops, SparseCore 0:
  10.8 74.7 reduce-scatter.4
  88.7 68.7 reduce-scatter.2
where the time goes:
time: 336 us; the launch traced here: 335 us
  blocking collectives  163 us (49%)
  waiting for transfers between devices  149 us (44%)
  between operations  16.2 us (5%)
  other arithmetic  5.36 us (2%)
    psum x1, blocking collectives, body(): squares = lax.psum(partial_value, ('group', 'shard'))  101 us
    reduce_scatter x1, waiting for transfers between devices, body(): lax.psum_scatter(exit_local, 'group', scatter_dimension=0, tiled=True)  77 us
    reduce_scatter x1, waiting for transfers between devices, body(): lax.psum_scatter(entry_local, 'group', scatter_dimension=0, tiled=True)  70.3 us
    all_gather x1, blocking collectives, body(): entry_weights = lax.all_gather(entry_round, 'group', axis=0, tiled=True)  31.3 us
    all_gather x1, blocking collectives, body(): exit_weights = lax.all_gather(exit_round, 'group', axis=0, tiled=True)  31 us
  transfers between devices with their start and end apart: 2, of which 2 were waited for; matrix products, arithmetic and copies ran while one was open for 0% of the time, Pallas kernels for 0%

commit v1 on v0

--- a/solution.py
+++ b/solution.py
@@ -21,6 +21,13 @@
     return (master, moment, variance)
 
 
+def sum_everywhere(values):
+    axes = ("group", "shard")
+    lanes = jnp.sum(values.reshape(-1, 128), axis=0)
+    sent = jnp.broadcast_to(lanes, (lax.axis_size(axes), 1, 128))
+    return jnp.sum(lax.all_to_all(sent, axes, 0, 0))
+
+
 def body(
     entry_grads,
     exit_grads,
@@ -37,12 +44,11 @@
     exit_width = exit_grads.shape[3]
     entry_local = entry_grads.reshape(entry_rows_dev, entry_width)
     exit_local = exit_grads.reshape(exit_rows_dev, exit_width)
-    entry_total, exit_total = (
-        lax.psum_scatter(entry_local, "group", scatter_dimension=0, tiled=True),
-        lax.psum_scatter(exit_local, "group", scatter_dimension=0, tiled=True),
-    )
-    partial_value = jnp.sum(entry_total * entry_total) + jnp.sum(exit_total * exit_total)
-    squares = lax.psum(partial_value, ("group", "shard"))
+    packed = jnp.concatenate([entry_local, exit_local], axis=1)
+    total = lax.psum_scatter(packed, "group", scatter_dimension=0, tiled=True)
+    entry_total = total[:, :entry_width]
+    exit_total = total[:, entry_width:]
+    squares = sum_everywhere(total * total)
     count = (entry_rows_dev * entry_width + exit_rows_dev * exit_width) * lax.axis_size("shard")
     limit = jnp.sqrt(jnp.float32(count))
     clip = jnp.minimum(jnp.float32(1.0), limit / (jnp.sqrt(squares) + 1e-06))

time: 336 us -> 205 us (0.61)
  waiting for transfers between devices: 149 us -> 78.8 us
  blocking collectives: 163 us -> 101 us
    psum x1 -> x0, blocking collectives: 101 us -> none  [body(): squares = lax.psum(partial_value, ('group', 'shard'))]
    reduce_scatter x2 -> x1, waiting for transfers between devices: 147 us -> 78.7 us  [body(): total = lax.psum_scatter(packed, 'group', scatter_dimension=0, tiled=True)]
    all_to_all x0 -> x1, blocking collectives: none -> 39.7 us  [sum_everywhere(): return jnp.sum(lax.all_to_all(sent, axes, 0, 0))]
  transfers between devices with their start and end apart: 2 -> 1, of which waited for: 2 -> 1; matrix products, arithmetic and copies ran while one was open for 0% -> 0% of each run, Pallas kernels for 0% -> 0%
where the time goes in v1:
time: 205 us; the launch traced here: 204 us
  blocking collectives  101 us (49%)
  waiting for transfers between devices  78.8 us (38%)
  between operations  14.8 us (7%)
  other arithmetic  7.27 us (4%)
    reduce_scatter x1, waiting for transfers between devices, body(): total = lax.psum_scatter(packed, 'group', scatter_dimension=0, tiled=True)  78.7 us
    all_to_all x1, blocking collectives, sum_everywhere(): return jnp.sum(lax.all_to_all(sent, axes, 0, 0))  39.7 us
    all_gather x1, blocking collectives, body(): entry_weights = lax.all_gather(entry_round, 'group', axis=0, tiled=True)  30.6 us
    all_gather x1, blocking collectives, body(): exit_weights = lax.all_gather(exit_round, 'group', axis=0, tiled=True)  30.5 us
  transfers between devices with their start and end apart: 1, of which 1 were waited for; matrix products, arithmetic and copies ran while one was open for 0% of the time, Pallas kernels for 0%

profile of v1, /device:TPU:6, one launch (start us, length us, event | category | flops | bytes accessed | tf_op | source)
XLA Modules:
  0.0 203.6 jit_solution(7940237761173604504)
XLA Ops:
  7.2 0.0 reduce-scatter.2.cloned.1.call-start
  7.2 3.2 %pad_maximum_fusion = f32[256,2304]{1,0:T(8,128)} fusion(f32[256,1024]{1,0:T(8,128)} %bitcast.67, f32[256,1280]{1,0:T(8,128)} %bitcast.65), kind=kLoop, calls=%fused_computation | loop fusion | flops 589824 | bytes 4718592 | tf_op jit(solution)/shard_map/concatenate | solution.py:47
  10.4 0.0 copy-start.2
  10.5 0.0 copy-start.3
  10.5 0.0 reduce-scatter.2.cloned.1.call-update
  10.5 78.7 %reduce-scatter.2.cloned.1.call-done = f32[16,2304]{1,0:T(8,128)} async-done(((f32[256,2304]{1,0:T(8,128)}), f32[16,2304]{1,0:T(8,128)}) %reduce-scatter.2.cloned.1.call-update) | async-done | bytes 147472 | tf_op jit(solution)/shard_map/reduce_scatter | solution.py:48
  89.2 1.1 mul.96
  90.3 0.1 reduce_sum.18
  90.4 0.1 broadcast_in_dim.27
  90.5 39.7 %all_to_all.5 = f32[512,1,128]{2,1,0:T(1,128)S(1)} all-to-all(f32[512,1,128]{2,1,0:T(1,128)S(1)} %broadcast_in_dim.27), channel_id=1, replica_groups=mesh['group'=16,'shard'=32] {'group','shard'}, dimensions={0} | all-to-all | bytes 524288 | tf_op jit(solution)/shard_map/all_to_all | solution.py:28
  130.2 0.7 reduce_sum.19
  131.6 0.0 copy-done.4
  131.6 0.0 copy-done.5
  131.6 0.0 copy-done.6
  131.7 1.5 fusion.10
  133.2 30.5 %all_gather.7 = bf16[256,1024]{1,0:T(8,128)(2,1)S(1)} all-gather(bf16[16,1024]{1,0:T(8,128)(2,1)S(1)} %get-tuple-element.8), channel_id=1, replica_groups=mesh['group'=16,'shard'=32] {'group'}, dimensions={0}, use_global_device_ids=true | all-gather | bytes 557056 | tf_op jit(solution)/shard_map/all_gather | solution.py:64
  163.7 0.0 copy-done.1
  163.7 0.0 copy-done.2
  163.7 0.0 copy-done.3
  163.7 0.0 copy-done
  163.7 0.7 fusion.11
  164.4 30.6 %all_gather.6 = bf16[256,1280]{1,0:T(8,128)(2,1)S(1)} all-gather(bf16[16,1280]{1,0:T(8,128)(2,1)S(1)} %get-tuple-element.10), channel_id=1, replica_groups=mesh['group'=16,'shard'=32] {'group'}, dimensions={0}, use_global_device_ids=true | all-gather | bytes 696320 | tf_op jit(solution)/shard_map/all_gather | solution.py:63
  195.1 0.8 copy.19
  195.9 0.8 copy.20
  (6 shorter events, 0.0 us)
Async XLA Ops:
  7.2 82.1 %reduce-scatter.2.cloned.1.call-start = ((), (), s32[]{:S(2)}) async-start(), calls=%async_computation.2 | async-start | bytes 2506752 | tf_op jit(solution)/shard_map/reduce_scatter | solution.py:48
  10.4 121.2 %copy-start.4 = (f32[1,16,1024]{2,1,0:T(8,128)S(1)}, f32[1,16,1024]{2,1,0:T(8,128)}, u32[]{:S(2)}) copy-start(f32[1,16,1024]{2,1,0:T(8,128)} %param.15) | copy-start | bytes 196612
  10.4 121.2 %copy-start.5 = (f32[1,16,1024]{2,1,0:T(8,128)S(1)}, f32[1,16,1024]{2,1,0:T(8,128)}, u32[]{:S(2)}) copy-start(f32[1,16,1024]{2,1,0:T(8,128)} %param.13) | copy-start | bytes 196612
  10.4 121.2 %copy-start.6 = (f32[1,16,1024]{2,1,0:T(8,128)S(1)}, f32[1,16,1024]{2,1,0:T(8,128)}, u32[]{:S(2)}) copy-start(f32[1,16,1024]{2,1,0:T(8,128)} %param.11) | copy-start | bytes 196612
  10.4 153.3 %copy-start.1 = (f32[1,16,1280]{2,1,0:T(8,128)S(1)}, f32[1,16,1280]{2,1,0:T(8,128)}, u32[]{:S(2)}) copy-start(f32[1,16,1280]{2,1,0:T(8,128)} %param.14) | copy-start | bytes 245764
  10.4 153.3 %copy-start.2 = (f32[1,16,1280]{2,1,0:T(8,128)S(1)}, f32[1,16,1280]{2,1,0:T(8,128)}, u32[]{:S(2)}) copy-start(f32[1,16,1280]{2,1,0:T(8,128)} %param.12) | copy-start | bytes 245764
  10.5 153.3 %copy-start.3 = (f32[1,16,1280]{2,1,0:T(8,128)S(1)}, f32[1,16,1280]{2,1,0:T(8,128)}, u32[]{:S(2)}) copy-start(f32[1,16,1280]{2,1,0:T(8,128)} %param.10) | copy-start | bytes 245764
  89.2 74.5 %copy-start = (f32[16,2304]{1,0:T(8,128)S(1)}, f32[16,2304]{1,0:T(8,128)}, u32[]{:S(2)}) copy-start(f32[16,2304]{1,0:T(8,128)} %reduce-scatter.2.cloned.1.call-done) | copy-start | bytes 442372
Sparse Core Ops, SparseCore 0:
  10.8 78.3 reduce-scatter.1

commit v2 on v0

v2 whole, which is shorter than its diff:
```python
import jax
import jax.numpy as jnp
from jax import lax
from jax.experimental import pallas as pl
from jax.experimental.pallas import tpu as pltpu
from jax.sharding import PartitionSpec as P

beta_first = 0.9
beta_second = 0.95
learn_rate = 0.01
decay_rate = 0.1
epsilon = 1e-08
correct_first = 1.0 - 0.9**40
correct_second = 1.0 - 0.95**40

LANES = 128
TILE = 8
ENTRY_PIECE = 640
EXIT_PIECE = 1024


def adamw_step(params, mean, square, total, clip):
    grads = clip * total
    moment = beta_first * mean + (1.0 - beta_first) * grads
    variance = beta_second * square + (1.0 - beta_second) * grads * grads
    update = moment / correct_first / (jnp.sqrt(variance / correct_second) + epsilon)
    master = params - learn_rate * (update + decay_rate * params)
    return (master, moment, variance)


def pieces_of(grads, width):
    rows, cols = grads.shape
    return [
        grads[r : r + TILE, c : c + width]
        for r in range(0, rows, TILE)
        for c in range(0, cols, width)
    ]


def join_kernel(places, *refs):
    piece_refs, (total_ref, lanes_ref) = refs[: len(places)], refs[len(places) :]
    sums = [jnp.zeros((TILE, LANES), jnp.float32) for _ in range(4)]
    turn = 0
    for (row, col), piece_ref in zip(places, piece_refs):
        for c in range(0, piece_ref.shape[1], LANES):
            values = piece_ref[:, c : c + LANES]
            total_ref[row : row + TILE, col + c : col + c + LANES] = values
            sums[turn % 4] = sums[turn % 4] + values * values
            turn += 1
    sums = (sums[0] + sums[1]) + (sums[2] + sums[3])
    lanes_ref[...] = jnp.sum(sums, axis=0, keepdims=True)


def join(entry_pieces, exit_pieces, rows, entry_width, exit_width):
    places = [(r, c) for r in range(0, rows, TILE) for c in range(0, entry_width, ENTRY_PIECE)]
    places += [
        (r, entry_width + c) for r in range(0, rows, TILE) for c in range(0, exit_width, EXIT_PIECE)
    ]
    return pl.pallas_call(
        lambda *refs: join_kernel(places, *refs),
        out_shape=(
            jax.ShapeDtypeStruct((rows, entry_width + exit_width), jnp.float32),
            jax.ShapeDtypeStruct((1, LANES), jnp.float32),
        ),
        name="join_totals",
    )(*entry_pieces, *exit_pieces)


def weights_kernel(rows, entry_width, scale_ref, state_ref, total_ref, entry_ref, exit_ref):
    along, squared = scale_ref[0, 0], scale_ref[0, 1]
    step = 2 * LANES
    for part in range(total_ref.shape[0] // rows):
        here = slice(part * rows, (part + 1) * rows)
        top = part * 3 * rows
        for c in range(0, total_ref.shape[1], step):
            cols = slice(c, c + step)
            total = total_ref[here, cols]
            ahead = state_ref[top + rows : top + 2 * rows, cols] + along * total
            spread = state_ref[top + 2 * rows : top + 3 * rows, cols] + squared * (total * total)
            master = state_ref[top : top + rows, cols] - ahead / (jnp.sqrt(spread) + epsilon)
            out_ref, at = (entry_ref, c) if c < entry_width else (exit_ref, c - entry_width)
            out_ref[here, at : at + step] = master.astype(out_ref.dtype)


def weights(scales, state, total, rows, entry_width, exit_width, parts):
    groups = total.shape[0] // rows
    high = rows * parts
    return pl.pallas_call(
        lambda *refs: weights_kernel(rows, entry_width, *refs),
        grid=(groups // parts,),
        in_specs=[
            pl.BlockSpec(memory_space=pltpu.SMEM),
            pl.BlockSpec((3 * high, total.shape[1]), lambda i: (i, 0)),
            pl.BlockSpec((high, total.shape[1]), lambda i: (i, 0)),
        ],
        out_specs=[
            pl.BlockSpec((high, entry_width), lambda i: (i, 0)),
            pl.BlockSpec((high, exit_width), lambda i: (i, 0)),
        ],
        out_shape=[
            jax.ShapeDtypeStruct((total.shape[0], entry_width), jnp.bfloat16),
            jax.ShapeDtypeStruct((total.shape[0], exit_width), jnp.bfloat16),
        ],
        name="all_weights",
    )(scales, state, total)


def body(
    entry_grads,
    exit_grads,
    entry_params,
    exit_params,
    entry_mean,
    exit_mean,
    entry_square,
    exit_square,
):
    rows, entry_width = entry_grads.shape[2:]
    exit_width = exit_grads.shape[3]
    own = entry_params.shape[1]
    state = jnp.concatenate(
        [
            jnp.concatenate([entry_params[0], exit_params[0]], 1) * (1.0 - learn_rate * decay_rate),
            jnp.concatenate([entry_mean[0], exit_mean[0]], 1)
            * (learn_rate * beta_first / correct_first),
            jnp.concatenate([entry_square[0], exit_square[0]], 1) * (beta_second / correct_second),
        ],
        axis=0,
    )
    all_state = lax.all_gather(state, "group", axis=0, tiled=True)

    entry_pieces = pieces_of(entry_grads.reshape(rows, entry_width), ENTRY_PIECE)
    exit_pieces = pieces_of(exit_grads.reshape(rows, exit_width), EXIT_PIECE)
    summed = lax.psum(entry_pieces + exit_pieces, "group")
    total, lanes = join(
        summed[: len(entry_pieces)], summed[len(entry_pieces) :], rows, entry_width, exit_width
    )
    shards = lax.axis_size("shard")
    sent = jnp.broadcast_to(lanes, (shards, 1, LANES))
    squares = jnp.sum(lax.all_to_all(sent, "shard", 0, 0))
    count = (rows * entry_width + rows * exit_width) * shards
    limit = jnp.sqrt(jnp.float32(count))
    clip = jnp.minimum(jnp.float32(1.0), limit / (jnp.sqrt(squares) + 1e-06))

    first = lax.axis_index("group") * own
    mine = lax.dynamic_slice_in_dim(total, first, own, axis=0)
    entry_master, entry_moment, entry_variance = adamw_step(
        entry_params[0], entry_mean[0], entry_square[0], mine[:, :entry_width], clip
    )
    exit_master, exit_moment, exit_variance = adamw_step(
        exit_params[0], exit_mean[0], exit_square[0], mine[:, entry_width:], clip
    )
    along = clip * (learn_rate * (1.0 - beta_first) / correct_first)
    squared = clip * clip * ((1.0 - beta_second) / correct_second)
    scales = jnp.stack([along, squared]).reshape(1, 2)
    entry_weights, exit_weights = weights(
        scales, all_state, total, own, entry_width, exit_width, parts=2
    )
    return (
        entry_master[None],
        exit_master[None],
        entry_moment[None],
        exit_moment[None],
        entry_variance[None],
        exit_variance[None],
        entry_weights[None],
        exit_weights[None],
    )


def solution(mesh):
    placed = (
        P("group", "shard", None, None),
        P("group", "shard", None, None),
        P("shard", "group", None),
        P("shard", "group", None),
        P("shard", "group", None),
        P("shard", "group", None),
        P("shard", "group", None),
        P("shard", "group", None),
    )
    return jax.shard_map(
        body,
        mesh=mesh,
        in_specs=placed,
        out_specs=(
            P("shard", "group", None),
            P("shard", "group", None),
            P("shard", "group", None),
            P("shard", "group", None),
            P("shard", "group", None),
            P("shard", "group", None),
            P("shard", None, None),
            P("shard", None, None),
        ),
        check_vma=False,
    )
```

time: 336 us -> 164 us (0.49)
  waiting for transfers between devices: 149 us -> 8.6 us
  blocking collectives: 163 us -> 111 us
  Pallas kernels: 0 us -> 10.7 us
  starting transfers between devices: 0.08 us -> 7.6 us
    reduce_scatter x2 -> x0, waiting for transfers between devices: 147 us -> none  [the longest x1 77 us: body(): lax.psum_scatter(exit_local, 'group', scatter_dimension=0, tiled=True)]
    all_gather x2 -> x0, blocking collectives: 62.3 us -> none  [the longest x1 31.3 us: body(): entry_weights = lax.all_gather(entry_round, 'group', axis=0, tiled=True)]
    pallas_call x0 -> x2, Pallas kernels: none -> 10.7 us  [the longest x1 7.25 us: weights(): pl.pallas_call(lambda *refs: weights_kernel(rows, entry_width, *refs), gr...]
    psum x1, blocking collectives: 101 us -> 111 us  [body(): summed = lax.psum(entry_pieces + exit_pieces, 'group')]
    all_to_all x0 -> x1, starting transfers between devices: none -> 7.56 us  [body(): squares = jnp.sum(lax.all_to_all(sent, 'shard', 0, 0))]
    all_to_all x0 -> x1, waiting for transfers between devices: none -> 5.44 us  [body(): squares = jnp.sum(lax.all_to_all(sent, 'shard', 0, 0))]
  transfers between devices with their start and end apart: 2 -> 2, of which waited for: 2 -> 2; matrix products, arithmetic and copies ran while one was open for 0% -> 4% of each run, Pallas kernels for 0% -> 2%
where the time goes in v2:
time: 164 us; the launch traced here: 163 us
  blocking collectives  111 us (68%)
  between operations  14.9 us (9%)
  Pallas kernels  10.7 us (7%)
  waiting for transfers between devices  8.6 us (5%)
  starting transfers between devices  7.6 us (5%)
  other arithmetic  7.32 us (4%)
  local copies, waits for them, and re-layouts  2.49 us (2%)
    psum x1, blocking collectives, body(): summed = lax.psum(entry_pieces + exit_pieces, 'group')  111 us
    all_to_all x1, starting transfers between devices, body(): squares = jnp.sum(lax.all_to_all(sent, 'shard', 0, 0))  7.56 us
    pallas_call x1, Pallas kernels, weights(): pl.pallas_call(lambda *refs: weights_kernel(rows, entry_width, *refs), gr...  7.25 us
    all_to_all x1, waiting for transfers between devices, body(): squares = jnp.sum(lax.all_to_all(sent, 'shard', 0, 0))  5.44 us
    pallas_call x1, Pallas kernels, join(): pl.pallas_call(lambda *refs: join_kernel(places, *refs), out_shape=(jax.S...  3.44 us
  transfers between devices with their start and end apart: 2, of which 2 were waited for; matrix products, arithmetic and copies ran while one was open for 4% of the time, Pallas kernels for 2%

profile of v2, /device:TPU:6, one launch (start us, length us, event | category | flops | bytes accessed | tf_op | source)
XLA Modules:
  0.0 162.8 jit_solution(14990981138496750132)
XLA Ops:
  7.2 0.0 copy-start
  7.2 0.0 all-gather.2.cloned.1.call-start
  7.2 1.0 maximum_multiply_fusion.2
  8.3 1.0 maximum_multiply_fusion
  9.3 0.8 pad_maximum_fusion
  10.1 0.0 all-gather.2.cloned.1.call-update
  10.1 0.0 copy-done
  10.1 0.0 copy-start.1
  10.3 1.1 copy-done.1
  11.4 0.1 slice_bitcast_fusion
  11.4 111.2 %all-reduce.2 = (f32[8,640]{1,0:T(8,128)}, f32[8,640]{1,0:T(8,128)}, f32[8,640]{1,0:T(8,128)}, f32[8,640]{1,0:T(8,128)}, f32[8,640]{1,0:T(8,128)}, /*index=5*/f3...) all-reduce(f32[8,640]{1,0:T(8,128)S(1)} %get-tuple-element.181, ...), channel_id=1, replica_groups=mesh['group'=16,'shard'=32] {'group'}, use_global_device_ids=true, to_apply=%region_0.0 | all-reduce | flops 589824 | bytes 4718592 | tf_op jit(solution)/shard_map/psum | solution.py:134
  122.7 0.0 copy-start.4
  122.7 3.4 %join_totals.1 = (f32[256,2304]{1,0:T(8,128)}, f32[1,128]{1,0:T(1,128)}) custom-call(f32[8,640]{1,0:T(8,128)} %get-tuple-element.16.refs_0_, f32[8,640]{1,0:T(8,128)} %get-tuple-element.17.refs_1_, f32[8,640]{1,0:T(8,128)} %get-tuple-element.18.refs_2_, f32[8,640]{1,0:T(8,128)} %get-tuple-element.19.refs_3_, f32[8,640]{1,0:T(8,128)} %get-tuple-element.20.refs_4_, ...), custom_call_target="tpu_custom_call" | custom-call | tf_op jit(solution)/shard_map/join_totals/pallas_call | solution.py:59
  126.1 1.2 broadcast_in_dim.27
  127.3 7.6 %all-to-all-start = ((f32[32,1,128]{2,1,0:T(1,128)}), f32[32,1,128]{2,1,0:T(1,128)S(1)}, u32[]{:S(2)}, u32[]{:S(2)}) async-start(f32[32,1,128]{2,1,0:T(1,128)} %broadcast_in_dim.27), calls=%async_computation | async-start | bytes 32768 | tf_op jit(solution)/shard_map/all_to_all | solution.py:140
  134.9 5.4 %all-to-all-done = f32[32,1,128]{2,1,0:T(1,128)S(1)} async-done(((f32[32,1,128]{2,1,0:T(1,128)}), f32[32,1,128]{2,1,0:T(1,128)S(1)}, u32[]{:S(2)}, u32[]{:S(2)}) %all-to-all-start) | async-done | bytes 16416 | tf_op jit(solution)/shard_map/all_to_all | solution.py:140
  140.3 0.6 reduce_sum.9
  141.7 0.7 maximum_bitcast_fusion.refs_0_
  142.3 0.0 copy-done.5
  142.3 1.6 fusion.5
  143.9 0.0 copy-done.4
  143.9 1.6 %fusion.4 = (f32[1,16,1280]{2,1,0:T(8,128)}, f32[1,16,1280]{2,1,0:T(8,128)}, f32[1,16,1280]{2,1,0:T(8,128)}) fusion(f32[256,2304]{1,0:T(8,128)} %get-tuple-element.13.refs_2_, s32[]{:T(128)S(6)} %select_n.3, f32[]{:T(128)S(6)} %min_shard_map.3, f32[1,16,1280]{2,1,0:T(8,128)S(1)} %copy-done.2, f32[1,16,1280]{2,1,0:T(8,128)S(1)} %copy-done.3, ...), kind=kLoop, calls=%fused_computation.48 | loop fusion | flops 327680 | bytes 573448 | tf_op jit(solution)/shard_map/broadcast_in_dim | solution.py:164
  145.6 3.1 %all-gather.2.cloned.1.call-done.refs_1_ = f32[768,2304]{1,0:T(8,128)} async-done(((f32[48,2304]{1,0:T(8,128)}), f32[768,2304]{1,0:T(8,128)}) %all-gather.2.cloned.1.call-update) | async-done | bytes 7077904 | tf_op jit(solution)/shard_map/all_gather | solution.py:130
  148.7 7.2 %all_weights.1 = (bf16[256,1280]{1,0:T(8,128)(2,1)}, bf16[256,1024]{1,0:T(8,128)(2,1)}) custom-call(f32[1,2]{1,0:T(1,128)} %maximum_bitcast_fusion.refs_0_, f32[768,2304]{1,0:T(8,128)} %all-gather.2.cloned.1.call-done.refs_1_, f32[256,2304]{1,0:T(8,128)} %get-tuple-element.13.refs_2_), custom_call_target="tpu_custom_call" | custom-call | tf_op jit(solution)/shard_map/all_weights/pallas_call | solution.py:88
  (14 shorter events, 0.2 us)
Async XLA Ops:
  7.2 2.9 %copy-start = (f32[1,1,256,1280]{3,2,1,0:T(8,128)S(1)}, f32[1,1,256,1280]{3,2,1,0:T(8,128)}, u32[]{:S(2)}) copy-start(f32[1,1,256,1280]{3,2,1,0:T(8,128)} %param.8) | copy-start | bytes 3932164
  7.2 141.5 %all-gather.2.cloned.1.call-start = ((), (), s32[]{:S(2)}) async-start(), calls=%async_computation.1 | async-start | bytes 7520256 | tf_op jit(solution)/shard_map/all_gather | solution.py:130
  10.1 1.2 copy-start.1
  122.6 19.7 %copy-start.5 = (f32[1,16,1024]{2,1,0:T(8,128)S(1)}, f32[1,16,1024]{2,1,0:T(8,128)}, u32[]{:S(2)}) copy-start(f32[1,16,1024]{2,1,0:T(8,128)} %param.13) | copy-start | bytes 196612
  122.6 19.7 %copy-start.6 = (f32[1,16,1024]{2,1,0:T(8,128)S(1)}, f32[1,16,1024]{2,1,0:T(8,128)}, u32[]{:S(2)}) copy-start(f32[1,16,1024]{2,1,0:T(8,128)} %param.11) | copy-start | bytes 196612
  122.6 19.7 %copy-start.7 = (f32[1,16,1024]{2,1,0:T(8,128)S(1)}, f32[1,16,1024]{2,1,0:T(8,128)}, u32[]{:S(2)}) copy-start(f32[1,16,1024]{2,1,0:T(8,128)} %param.15) | copy-start | bytes 196612
  122.6 21.3 %copy-start.2 = (f32[1,16,1280]{2,1,0:T(8,128)S(1)}, f32[1,16,1280]{2,1,0:T(8,128)}, u32[]{:S(2)}) copy-start(f32[1,16,1280]{2,1,0:T(8,128)} %param.14) | copy-start | bytes 245764
  122.6 21.3 %copy-start.3 = (f32[1,16,1280]{2,1,0:T(8,128)S(1)}, f32[1,16,1280]{2,1,0:T(8,128)}, u32[]{:S(2)}) copy-start(f32[1,16,1280]{2,1,0:T(8,128)} %param.12) | copy-start | bytes 245764
  122.7 21.3 %copy-start.4 = (f32[1,16,1280]{2,1,0:T(8,128)S(1)}, f32[1,16,1280]{2,1,0:T(8,128)}, u32[]{:S(2)}) copy-start(f32[1,16,1280]{2,1,0:T(8,128)} %param.10) | copy-start | bytes 245764
  127.3 13.0 %all-to-all-start = ((f32[32,1,128]{2,1,0:T(1,128)}), f32[32,1,128]{2,1,0:T(1,128)S(1)}, u32[]{:S(2)}, u32[]{:S(2)}) async-start(f32[32,1,128]{2,1,0:T(1,128)} %broadcast_in_dim.27), calls=%async_computation | async-start | bytes 32768 | tf_op jit(solution)/shard_map/all_to_all | solution.py:140
Sparse Core Ops, SparseCore 0:
  10.7 137.9 all-gather.1

commit v3 on v0

v3 whole, which is shorter than its diff:
```python
import jax
import jax.numpy as jnp
from jax import lax
from jax.experimental import pallas as pl
from jax.experimental.pallas import tpu as pltpu
from jax.sharding import PartitionSpec as P

beta_first = 0.9
beta_second = 0.95
learn_rate = 0.01
decay_rate = 0.1
epsilon = 1e-08
correct_first = 1.0 - 0.9**40
correct_second = 1.0 - 0.95**40

LANES = 128
TILE = 8
ENTRY_PIECE = 640
EXIT_PIECE = 1024
NEAR = 4


def pieces_of(grads, width):
    rows, cols = grads.shape
    return [
        grads[r : r + TILE, c : c + width]
        for r in range(0, rows, TILE)
        for c in range(0, cols, width)
    ]


def places_of(rows, cols, width, start):
    return [(r, start + c) for r in range(0, rows, TILE) for c in range(0, cols, width)]


def own_and_squares_kernel(places, own, me_ref, *refs):
    piece_refs, (own_ref, lanes_ref) = refs[: len(places)], refs[len(places) :]
    me = me_ref[0, 0]
    sums = [jnp.zeros((TILE, LANES), jnp.float32) for _ in range(4)]
    turn = 0
    for piece_ref in piece_refs:
        for c in range(0, piece_ref.shape[1], LANES):
            values = piece_ref[:, c : c + LANES]
            sums[turn % 4] = sums[turn % 4] + values * values
            turn += 1
    sums = (sums[0] + sums[1]) + (sums[2] + sums[3])
    lanes = jnp.sum(sums, axis=0, keepdims=True)
    lanes_ref[...] = jnp.broadcast_to(lanes[None], lanes_ref.shape)
    for block in sorted({row // own for row, _ in places}):

        @pl.when(me == block)
        def _(block=block):
            for (row, col), piece_ref in zip(places, piece_refs):
                if row // own == block:
                    top = row - block * own
                    own_ref[top : top + TILE, col : col + piece_ref.shape[1]] = piece_ref[...]


def own_and_squares(pieces, places, own, width, shards):
    me = lax.axis_index("group").reshape(1, 1)
    return pl.pallas_call(
        lambda *refs: own_and_squares_kernel(places, own, *refs),
        in_specs=[pl.BlockSpec(memory_space=pltpu.SMEM)]
        + [pl.BlockSpec(memory_space=pltpu.VMEM) for _ in pieces],
        out_shape=(
            jax.ShapeDtypeStruct((own, width), jnp.float32),
            jax.ShapeDtypeStruct((shards, 1, LANES), jnp.float32),
        ),
        name="own_and_squares",
    )(me, *pieces)


def update_kernel(limit, entry_width, refs):
    squares_ref, total_ref = refs[:2]
    states, outs, round_ref = refs[2:8], refs[8:14], refs[14]
    squares = jnp.sum(jnp.sum(squares_ref[...], axis=0), axis=1, keepdims=True)
    clip = jnp.minimum(jnp.float32(1.0), limit / (jnp.sqrt(squares) + 1e-06))
    for side, start in ((0, 0), (1, entry_width)):
        params_ref, mean_ref, square_ref = states[side], states[2 + side], states[4 + side]
        for c in range(0, params_ref.shape[2], 2 * LANES):
            cols = slice(c, c + 2 * LANES)
            there = slice(start + c, start + c + 2 * LANES)
            params = params_ref[0, :, cols]
            grads = clip * total_ref[:, there]
            moment = beta_first * mean_ref[0, :, cols] + (1.0 - beta_first) * grads
            variance = beta_second * square_ref[0, :, cols] + (1.0 - beta_second) * grads * grads
            update = moment / correct_first / (jnp.sqrt(variance / correct_second) + epsilon)
            master = params - learn_rate * (update + decay_rate * params)
            outs[side][0, :, cols] = master
            outs[2 + side][0, :, cols] = moment
            outs[4 + side][0, :, cols] = variance
            round_ref[:, there] = master.astype(round_ref.dtype)


def update(squares, total, states, limit, entry_width):
    return pl.pallas_call(
        lambda *refs: update_kernel(limit, entry_width, refs),
        out_shape=[jax.ShapeDtypeStruct(s.shape, s.dtype) for s in states]
        + [jax.ShapeDtypeStruct(total.shape, jnp.bfloat16)],
        name="own_update",
    )(squares, total, *states)


def place_kernel(own, entry_width, me_ref, own_ref, ahead_ref, across_ref, after_ref, behind_ref, entry_ref, exit_ref):
    me = me_ref[0, 0]
    half = across_ref.shape[1]
    for residue in range(NEAR):
        for turn in range(NEAR):

            @pl.when(lax.rem(me + turn, NEAR) == residue)
            def _(residue=residue, turn=turn):
                for block in range(own_ref.shape[0] // own):
                    src = slice(block * own, (block + 1) * own)
                    top = (block * NEAR + residue) * own
                    dst = slice(top, top + own)
                    for out_ref, start in ((entry_ref, 0), (exit_ref, entry_width)):
                        end = start + out_ref.shape[1]
                        if turn != 2:
                            ref = (own_ref, ahead_ref, None, behind_ref)[turn]
                            out_ref[dst, :] = ref[src, start:end]
                            continue
                        if start < half:
                            stop = min(half, end)
                            out_ref[dst, : stop - start] = across_ref[src, start:stop]
                        if end > half:
                            low = max(half, start)
                            out_ref[dst, low - start :] = after_ref[src, low - half : end - half]


def share(rounded, entry_width):
    groups = lax.axis_size("group")
    own, width = rounded.shape
    far = groups // NEAR
    half = width // 2
    strides = [[r + NEAR * a for a in range(far)] for r in range(NEAR)]
    gathered = lax.all_gather(rounded, "group", axis=0, tiled=True, axis_index_groups=strides)

    def moved(values, by):
        return lax.ppermute(values, "group", [(i, (i + by) % groups) for i in range(groups)])

    ahead, behind = moved(gathered, -1), moved(gathered, 1)
    across, after = moved(gathered[:, :half], 2), moved(gathered[:, half:], -2)
    me = lax.axis_index("group").reshape(1, 1)
    vmem = pl.BlockSpec(memory_space=pltpu.VMEM)
    return pl.pallas_call(
        lambda *refs: place_kernel(own, entry_width, *refs),
        in_specs=[pl.BlockSpec(memory_space=pltpu.SMEM)] + [vmem] * 5,
        out_shape=[
            jax.ShapeDtypeStruct((groups * own, entry_width), rounded.dtype),
            jax.ShapeDtypeStruct((groups * own, width - entry_width), rounded.dtype),
        ],
        name="place_weights",
    )(me, gathered, ahead, across, after, behind)


def body(
    entry_grads,
    exit_grads,
    entry_params,
    exit_params,
    entry_mean,
    exit_mean,
    entry_square,
    exit_square,
):
    rows, entry_width = entry_grads.shape[2:]
    exit_width = exit_grads.shape[3]
    own = entry_params.shape[1]
    shards = lax.axis_size("shard")
    pieces = pieces_of(entry_grads.reshape(rows, entry_width), ENTRY_PIECE)
    pieces += pieces_of(exit_grads.reshape(rows, exit_width), EXIT_PIECE)
    places = places_of(rows, entry_width, ENTRY_PIECE, 0)
    places += places_of(rows, exit_width, EXIT_PIECE, entry_width)
    summed = lax.psum(pieces, "group")
    total, lanes = own_and_squares(summed, places, own, entry_width + exit_width, shards)
    squares = lax.all_to_all(lanes, "shard", 0, 0)
    limit = ((rows * entry_width + rows * exit_width) * shards) ** 0.5
    states = (entry_params, exit_params, entry_mean, exit_mean, entry_square, exit_square)
    *outs, rounded = update(squares, total, states, limit, entry_width)
    entry_weights, exit_weights = share(rounded, entry_width)
    return (*outs, entry_weights[None], exit_weights[None])


def solution(mesh):
    placed = (
        P("group", "shard", None, None),
        P("group", "shard", None, None),
        P("shard", "group", None),
        P("shard", "group", None),
        P("shard", "group", None),
        P("shard", "group", None),
        P("shard", "group", None),
        P("shard", "group", None),
    )
    return jax.shard_map(
        body,
        mesh=mesh,
        in_specs=placed,
        out_specs=(
            P("shard", "group", None),
            P("shard", "group", None),
            P("shard", "group", None),
            P("shard", "group", None),
            P("shard", "group", None),
            P("shard", "group", None),
            P("shard", None, None),
            P("shard", None, None),
        ),
        check_vma=False,
    )
```

time: 336 us -> 154 us (0.46)
  waiting for transfers between devices: 149 us -> 6.23 us
  blocking collectives: 163 us -> 118 us
  between operations: 16.2 us -> 0.75 us
  starting transfers between devices: 0.08 us -> 13.8 us
  Pallas kernels: 0 us -> 6.99 us
  other arithmetic: 5.36 us -> 0 us
  local copies, waits for them, and re-layouts: 1.66 us -> 5.43 us
    reduce_scatter x2 -> x0, waiting for transfers between devices: 147 us -> none  [the longest x1 77 us: body(): lax.psum_scatter(exit_local, 'group', scatter_dimension=0, tiled=True)]
    all_gather x2 -> x1, blocking collectives: 62.3 us -> 21 us  [share(): lax.all_gather(rounded, 'group', axis=0, tiled=True, axis_index_groups=st...]
    psum x1, blocking collectives: 101 us -> 84.1 us  [body(): summed = lax.psum(pieces, 'group')]
    ppermute x0 -> x4, starting transfers between devices: none -> 13.8 us  [moved(): lax.ppermute(values, 'group', [(i, (i + by) % groups) for i in range(grou...]
    all_to_all x0 -> x1, blocking collectives: none -> 13.1 us  [body(): squares = lax.all_to_all(lanes, 'shard', 0, 0)]
    pallas_call x0 -> x3, Pallas kernels: none -> 6.99 us  [the longest x1 2.51 us: own_and_squares(): pl.pallas_call(lambda *refs: own_and_squares_kernel(places, own, *refs),...]
    ppermute x0 -> x4, waiting for transfers between devices: none -> 6.23 us  [moved(): lax.ppermute(values, 'group', [(i, (i + by) % groups) for i in range(grou...]
    slice x0 -> x7, local copies, waits for them, and re-layouts: none -> 3.94 us  [the longest x6 3.92 us: pieces_of(): grads[r:r + TILE, c:c + width]]
  transfers between devices with their start and end apart: 2 -> 4, of which waited for: 2 -> 2; matrix products, arithmetic and copies ran while one was open for 0% -> 0% of each run, Pallas kernels for 0% -> 0%
where the time goes in v3:
time: 154 us; the launch traced here: 151 us
  blocking collectives  118 us (77%)
  starting transfers between devices  13.8 us (9%)
  Pallas kernels  6.99 us (5%)
  waiting for transfers between devices  6.23 us (4%)
  local copies, waits for them, and re-layouts  5.43 us (4%)
    psum x1, blocking collectives, body(): summed = lax.psum(pieces, 'group')  84.1 us
    all_gather x1, blocking collectives, share(): lax.all_gather(rounded, 'group', axis=0, tiled=True, axis_index_groups=st...  21 us
    ppermute x4, starting transfers between devices, moved(): lax.ppermute(values, 'group', [(i, (i + by) % groups) for i in range(grou...  13.8 us
    all_to_all x1, blocking collectives, body(): squares = lax.all_to_all(lanes, 'shard', 0, 0)  13.1 us
    ppermute x4, waiting for transfers between devices, moved(): lax.ppermute(values, 'group', [(i, (i + by) % groups) for i in range(grou...  6.23 us
    slice x6, local copies, waits for them, and re-layouts, pieces_of(): grads[r:r + TILE, c:c + width]  3.92 us
  transfers between devices with their start and end apart: 4, of which 2 were waited for; matrix products, arithmetic and copies ran while one was open for 0% of the time, Pallas kernels for 0%

profile of v3, /device:TPU:6, one launch (start us, length us, event | category | flops | bytes accessed | tf_op | source)
XLA Modules:
  0.0 151.4 jit_solution(5663213380320368374)
XLA Ops:
  0.6 1.0 fusion
  1.7 1.0 fusion.1
  2.7 1.0 fusion.2
  3.6 0.0 copy-done.1
  3.6 0.1 slice_bitcast_fusion
  3.8 0.8 fusion.3
  4.6 84.1 %all-reduce.2 = (f32[8,640]{1,0:T(8,128)}, f32[8,640]{1,0:T(8,128)}, f32[8,640]{1,0:T(8,128)}, f32[8,640]{1,0:T(8,128)}, f32[8,640]{1,0:T(8,128)}, /*index=5*/f3...) all-reduce(f32[8,640]{1,0:T(8,128)S(1)} %get-tuple-element.189, ...), channel_id=1, replica_groups=mesh['group'=16,'shard'=32] {'group'}, use_global_device_ids=true, to_apply=%region_0.0 | all-reduce | flops 589824 | bytes 4718592 | tf_op jit(solution)/shard_map/psum | solution.py:174
  88.7 2.5 %own_and_squares.1 = (f32[16,2304]{1,0:T(8,128)}, f32[32,1,128]{2,1,0:T(1,128)}) custom-call(s32[1,1]{1,0:T(1,128)} %bitcast.refs_0_, f32[8,640]{1,0:T(8,128)} %get-tuple-element.30.refs_1_, f32[8,640]{1,0:T(8,128)} %get-tuple-element.31.refs_2_, f32[8,640]{1,0:T(8,128)} %get-tuple-element.32.refs_3_, f32[8,640]{1,0:T(8,128)} %get-tuple-element.33.refs_4_, ...), custom_call_target="tpu_custom_call" | custom-call | tf_op jit(solution)/shard_map/own_and_squares/pallas_call | solution.py:61
  91.2 13.1 %all_to_all.5.refs_0_ = f32[32,1,128]{2,1,0:T(1,128)} all-to-all(f32[32,1,128]{2,1,0:T(1,128)} %get-tuple-element.19), channel_id=1, replica_groups=mesh['group'=16,'shard'=32] {'shard'}, dimensions={0} | all-to-all | bytes 32768 | tf_op jit(solution)/shard_map/all_to_all | solution.py:176
  104.3 2.1 %own_update.1 = (f32[1,16,1280]{2,1,0:T(8,128)}, f32[1,16,1024]{2,1,0:T(8,128)}, f32[1,16,1280]{2,1,0:T(8,128)}, f32[1,16,1024]{2,1,0:T(8,128)}, f32[1,16,1280]{...) custom-call(f32[32,1,128]{2,1,0:T(1,128)} %all_to_all.5.refs_0_, f32[16,2304]{1,0:T(8,128)} %get-tuple-element.20.refs_1_, ...), custom_call_target="tpu_custom_call" | custom-call | tf_op jit(solution)/shard_map/own_update/pallas_call | solution.py:96
  106.4 21.0 %all_gather.3.refs_1_ = bf16[64,2304]{1,0:T(8,128)(2,1)S(1)} all-gather(bf16[16,2304]{1,0:T(8,128)(2,1)} %get-tuple-element.27), channel_id=1, replica_groups={{0,128,256,384},{32,160,288,416},{64,192,320,448},{96,224,352,480},{1,1..., dimensions={0}, use_global_device_ids=true | all-gather | bytes 368640 | tf_op jit(solution)/shard_map/all_gather | solution.py:136
  127.4 1.9 %collective-permute-start = (bf16[64,2304]{1,0:T(8,128)(2,1)S(1)}, bf16[64,2304]{1,0:T(8,128)(2,1)S(1)}, u32[]{:S(2)}, u32[]{:S(2)}) collective-permute-start(bf16[64,2304]{1,0:T(8,128)(2,1)S(1)} %all_gather.3.refs_1_), channel_id=1, source_target_pairs={{0,480},{32,0},{64,32},{96,64},{128,96},{160,128},{192,160},{224,1... | collective-permute-start | bytes 884744 | tf_op jit(solution)/shard_map/ppermute | solution.py:139
  129.3 3.9 %collective-permute-start.3 = (bf16[64,2304]{1,0:T(8,128)(2,1)S(1)}, bf16[64,2304]{1,0:T(8,128)(2,1)S(1)}, u32[]{:S(2)}, u32[]{:S(2)}) collective-permute-start(bf16[64,2304]{1,0:T(8,128)(2,1)S(1)} %all_gather.3.refs_1_), channel_id=1, source_target_pairs={{0,32},{32,64},{64,96},{96,128},{128,160},{160,192},{192,224},{224... | collective-permute-start | bytes 884744 | tf_op jit(solution)/shard_map/ppermute | solution.py:139
  133.3 1.9 %collective-permute-start.1 = (bf16[64,1152]{1,0:T(8,128)(2,1)S(1)}, bf16[64,1152]{1,0:T(8,128)(2,1)S(1)}, u32[]{:S(2)}, u32[]{:S(2)}) collective-permute-start(bf16[64,1152]{1,0:T(8,128)(2,1)S(1)} %get-tuple-element.223), channel_id=1, source_target_pairs={{0,64},{32,96},{64,128},{96,160},{128,192},{160,224},{192,256},{22... | collective-permute-start | bytes 442376 | tf_op jit(solution)/shard_map/ppermute | solution.py:139
  135.2 6.0 %collective-permute-start.2 = (bf16[64,1152]{1,0:T(8,128)(2,1)S(1)}, bf16[64,1152]{1,0:T(8,128)(2,1)S(1)}, u32[]{:S(2)}, u32[]{:S(2)}) collective-permute-start(bf16[64,1152]{1,0:T(8,128)(2,1)S(1)} %get-tuple-element.222), channel_id=1, source_target_pairs={{0,448},{32,480},{64,0},{96,32},{128,64},{160,96},{192,128},{224,1... | collective-permute-start | bytes 442376 | tf_op jit(solution)/shard_map/ppermute | solution.py:139
  141.3 1.9 %collective-permute-done.1.refs_3_ = bf16[64,1152]{1,0:T(8,128)(2,1)S(1)} collective-permute-done((bf16[64,1152]{1,0:T(8,128)(2,1)S(1)}, bf16[64,1152]{1,0:T(8,128)(2,1)S(1)}, u32[]{:S(2)}, u32[]{:S(2)}) %collective-permute-start.1) | collective-permute-done | bytes 147488 | tf_op jit(solution)/shard_map/ppermute | solution.py:139
  143.2 4.3 %collective-permute-done.2.refs_4_ = bf16[64,1152]{1,0:T(8,128)(2,1)S(1)} collective-permute-done((bf16[64,1152]{1,0:T(8,128)(2,1)S(1)}, bf16[64,1152]{1,0:T(8,128)(2,1)S(1)}, u32[]{:S(2)}, u32[]{:S(2)}) %collective-permute-start.2) | collective-permute-done | bytes 147488 | tf_op jit(solution)/shard_map/ppermute | solution.py:139
  147.5 0.0 collective-permute-done.refs_2_
  147.5 0.0 collective-permute-done.3.refs_5_
  147.5 0.0 copy-done
  147.5 0.6 copy-done.5
  148.2 0.1 copy-done.2
  148.3 0.7 copy-done.3
  149.0 2.4 %place_weights.1 = (bf16[256,1280]{1,0:T(8,128)(2,1)}, bf16[256,1024]{1,0:T(8,128)(2,1)}) custom-call(s32[1,1]{1,0:T(1,128)} %bitcast.refs_0_, bf16[64,2304]{1,0:T(8,128)(2,1)} %copy-done, bf16[64,2304]{1,0:T(8,128)(2,1)} %copy-done.2, bf16[64,1152]{1,0:T(8,128)(2,1)} %copy-done.4, bf16[64,1152]{1,0:T(8,128)(2,1)} %copy-done.5, bf16[64,2304]{1,0:T(8,128)(2,1)} %copy-done.3), custom_call_target="tpu_custom_call" | custom-call | tf_op jit(solution)/shard_map/place_weights/pallas_call | solution.py:145
  (9 shorter events, 0.1 us)
Async XLA Ops:
  0.6 3.0 %copy-start.1 = (f32[1,1,256,1024]{3,2,1,0:T(8,128)S(1)}, f32[1,1,256,1024]{3,2,1,0:T(8,128)}, u32[]{:S(2)}) copy-start(f32[1,1,256,1024]{3,2,1,0:T(8,128)} %param.9) | copy-start | bytes 3145732
  127.4 20.1 %copy-start = (bf16[64,2304]{1,0:T(8,128)(2,1)}, bf16[64,2304]{1,0:T(8,128)(2,1)S(1)}, u32[]{:S(2)}) copy-start(bf16[64,2304]{1,0:T(8,128)(2,1)S(1)} %all_gather.3.refs_1_) | copy-start | bytes 884740
  127.4 20.1 %collective-permute-start = (bf16[64,2304]{1,0:T(8,128)(2,1)S(1)}, bf16[64,2304]{1,0:T(8,128)(2,1)S(1)}, u32[]{:S(2)}, u32[]{:S(2)}) collective-permute-start(bf16[64,2304]{1,0:T(8,128)(2,1)S(1)} %all_gather.3.refs_1_), channel_id=1, source_target_pairs={{0,480},{32,0},{64,32},{96,64},{128,96},{160,128},{192,160},{224,1... | collective-permute-start | bytes 884744 | tf_op jit(solution)/shard_map/ppermute | solution.py:139
  129.3 18.2 %collective-permute-start.3 = (bf16[64,2304]{1,0:T(8,128)(2,1)S(1)}, bf16[64,2304]{1,0:T(8,128)(2,1)S(1)}, u32[]{:S(2)}, u32[]{:S(2)}) collective-permute-start(bf16[64,2304]{1,0:T(8,128)(2,1)S(1)} %all_gather.3.refs_1_), channel_id=1, source_target_pairs={{0,32},{32,64},{64,96},{96,128},{128,160},{160,192},{192,224},{224... | collective-permute-start | bytes 884744 | tf_op jit(solution)/shard_map/ppermute | solution.py:139
  133.3 9.9 %collective-permute-start.1 = (bf16[64,1152]{1,0:T(8,128)(2,1)S(1)}, bf16[64,1152]{1,0:T(8,128)(2,1)S(1)}, u32[]{:S(2)}, u32[]{:S(2)}) collective-permute-start(bf16[64,1152]{1,0:T(8,128)(2,1)S(1)} %get-tuple-element.223), channel_id=1, source_target_pairs={{0,64},{32,96},{64,128},{96,160},{128,192},{160,224},{192,256},{22... | collective-permute-start | bytes 442376 | tf_op jit(solution)/shard_map/ppermute | solution.py:139
  135.2 12.3 %collective-permute-start.2 = (bf16[64,1152]{1,0:T(8,128)(2,1)S(1)}, bf16[64,1152]{1,0:T(8,128)(2,1)S(1)}, u32[]{:S(2)}, u32[]{:S(2)}) collective-permute-start(bf16[64,1152]{1,0:T(8,128)(2,1)S(1)} %get-tuple-element.222), channel_id=1, source_target_pairs={{0,448},{32,480},{64,0},{96,32},{128,64},{160,96},{192,128},{224,1... | collective-permute-start | bytes 442376 | tf_op jit(solution)/shard_map/ppermute | solution.py:139
  143.2 4.3 %copy-start.4 = (bf16[64,1152]{1,0:T(8,128)(2,1)}, bf16[64,1152]{1,0:T(8,128)(2,1)S(1)}, u32[]{:S(2)}) copy-start(bf16[64,1152]{1,0:T(8,128)(2,1)S(1)} %collective-permute-done.1.refs_3_) | copy-start | bytes 442372
  147.5 0.7 copy-start.5
  147.5 0.8 copy-start.2
  148.3 0.7 copy-start.3

commit v4 on v3

--- a/solution.py
+++ b/solution.py
@@ -70,68 +70,59 @@
     )(me, *pieces)
 
 
-def update_kernel(limit, entry_width, refs):
+def clip_of(squares_ref, limit):
+    squares = jnp.sum(jnp.sum(squares_ref[...], axis=0), axis=1, keepdims=True)
+    return jnp.minimum(jnp.float32(1.0), limit / (jnp.sqrt(squares) + 1e-06))
+
+
+def adamw_step(params, mean, square, total, clip):
+    grads = clip * total
+    moment = beta_first * mean + (1.0 - beta_first) * grads
+    variance = beta_second * square + (1.0 - beta_second) * grads * grads
+    update = moment / correct_first / (jnp.sqrt(variance / correct_second) + epsilon)
+    master = params - learn_rate * (update + decay_rate * params)
+    return (master, moment, variance)
+
+
+def update_kernel(limit, entry_width, keep, refs):
     squares_ref, total_ref = refs[:2]
-    states, outs, round_ref = refs[2:8], refs[8:14], refs[14]
-    squares = jnp.sum(jnp.sum(squares_ref[...], axis=0), axis=1, keepdims=True)
-    clip = jnp.minimum(jnp.float32(1.0), limit / (jnp.sqrt(squares) + 1e-06))
+    states, outs = refs[2:8], refs[8:]
+    clip = clip_of(squares_ref, limit)
     for side, start in ((0, 0), (1, entry_width)):
         params_ref, mean_ref, square_ref = states[side], states[2 + side], states[4 + side]
         for c in range(0, params_ref.shape[2], 2 * LANES):
             cols = slice(c, c + 2 * LANES)
             there = slice(start + c, start + c + 2 * LANES)
-            params = params_ref[0, :, cols]
-            grads = clip * total_ref[:, there]
-            moment = beta_first * mean_ref[0, :, cols] + (1.0 - beta_first) * grads
-            variance = beta_second * square_ref[0, :, cols] + (1.0 - beta_second) * grads * grads
-            update = moment / correct_first / (jnp.sqrt(variance / correct_second) + epsilon)
-            master = params - learn_rate * (update + decay_rate * params)
-            outs[side][0, :, cols] = master
-            outs[2 + side][0, :, cols] = moment
-            outs[4 + side][0, :, cols] = variance
-            round_ref[:, there] = master.astype(round_ref.dtype)
-
-
-def update(squares, total, states, limit, entry_width):
+            stepped = adamw_step(
+                params_ref[0, :, cols],
+                mean_ref[0, :, cols],
+                square_ref[0, :, cols],
+                total_ref[:, there],
+                clip,
+            )
+            if keep:
+                for kind, values in enumerate(stepped):
+                    outs[2 * kind + side][0, :, cols] = values
+            else:
+                outs[0][:, there] = stepped[0].astype(outs[0].dtype)
+
+
+def update(squares, total, states, limit, entry_width, keep):
+    if keep:
+        shapes = [jax.ShapeDtypeStruct(s.shape, s.dtype) for s in states]
+    else:
+        shapes = [jax.ShapeDtypeStruct(total.shape, jnp.bfloat16)]
     return pl.pallas_call(
-        lambda *refs: update_kernel(limit, entry_width, refs),
-        out_shape=[jax.ShapeDtypeStruct(s.shape, s.dtype) for s in states]
-        + [jax.ShapeDtypeStruct(total.shape, jnp.bfloat16)],
-        name="own_update",
+        lambda *refs: update_kernel(limit, entry_width, keep, refs),
+        out_shape=shapes,
+        name="own_state" if keep else "own_weights",
     )(squares, total, *states)
-
-
-def place_kernel(own, entry_width, me_ref, own_ref, ahead_ref, across_ref, after_ref, behind_ref, entry_ref, exit_ref):
-    me = me_ref[0, 0]
-    half = across_ref.shape[1]
-    for residue in range(NEAR):
-        for turn in range(NEAR):
-
-            @pl.when(lax.rem(me + turn, NEAR) == residue)
-            def _(residue=residue, turn=turn):
-                for block in range(own_ref.shape[0] // own):
-                    src = slice(block * own, (block + 1) * own)
-                    top = (block * NEAR + residue) * own
-                    dst = slice(top, top + own)
-                    for out_ref, start in ((entry_ref, 0), (exit_ref, entry_width)):
-                        end = start + out_ref.shape[1]
-                        if turn != 2:
-                            ref = (own_ref, ahead_ref, None, behind_ref)[turn]
-                            out_ref[dst, :] = ref[src, start:end]
-                            continue
-                        if start < half:
-                            stop = min(half, end)
-                            out_ref[dst, : stop - start] = across_ref[src, start:stop]
-                        if end > half:
-                            low = max(half, start)
-                            out_ref[dst, low - start :] = after_ref[src, low - half : end - half]
 
 
 def share(rounded, entry_width):
     groups = lax.axis_size("group")
     own, width = rounded.shape
     far = groups // NEAR
-    half = width // 2
     strides = [[r + NEAR * a for a in range(far)] for r in range(NEAR)]
     gathered = lax.all_gather(rounded, "group", axis=0, tiled=True, axis_index_groups=strides)
 
@@ -139,18 +130,23 @@
         return lax.ppermute(values, "group", [(i, (i + by) % groups) for i in range(groups)])
 
     ahead, behind = moved(gathered, -1), moved(gathered, 1)
-    across, after = moved(gathered[:, :half], 2), moved(gathered[:, half:], -2)
-    me = lax.axis_index("group").reshape(1, 1)
-    vmem = pl.BlockSpec(memory_space=pltpu.VMEM)
-    return pl.pallas_call(
-        lambda *refs: place_kernel(own, entry_width, *refs),
-        in_specs=[pl.BlockSpec(memory_space=pltpu.SMEM)] + [vmem] * 5,
-        out_shape=[
-            jax.ShapeDtypeStruct((groups * own, entry_width), rounded.dtype),
-            jax.ShapeDtypeStruct((groups * own, width - entry_width), rounded.dtype),
-        ],
-        name="place_weights",
-    )(me, gathered, ahead, across, after, behind)
+    across = (moved(gathered[:, :entry_width], 2), moved(gathered[:, entry_width:], -2))
+    me = lax.axis_index("group").astype(jnp.uint32)
+
+    def placed(nearby, cols):
+        shape = (far, NEAR, own, cols)
+        residue = lax.broadcasted_iota(jnp.uint32, shape, 1)
+        out = nearby[0].reshape(far, 1, own, cols)
+        for turn in range(1, NEAR):
+            here = residue == ((me + turn) & (NEAR - 1))
+            out = jnp.where(here, nearby[turn].reshape(far, 1, own, cols), out)
+        return out.reshape(groups * own, cols)
+
+    sides = ((slice(0, entry_width), across[0]), (slice(entry_width, width), across[1]))
+    return gathered, [
+        placed((gathered[:, cols], ahead[:, cols], middle, behind[:, cols]), middle.shape[1])
+        for cols, middle in sides
+    ]
 
 
 def body(
@@ -176,8 +172,10 @@
     squares = lax.all_to_all(lanes, "shard", 0, 0)
     limit = ((rows * entry_width + rows * exit_width) * shards) ** 0.5
     states = (entry_params, exit_params, entry_mean, exit_mean, entry_square, exit_square)
-    *outs, rounded = update(squares, total, states, limit, entry_width)
-    entry_weights, exit_weights = share(rounded, entry_width)
+    (rounded,) = update(squares, total, states, limit, entry_width, keep=False)
+    gathered, (entry_weights, exit_weights) = share(rounded, entry_width)
+    squares, gathered = lax.optimization_barrier((squares, gathered))
+    outs = update(squares, total, states, limit, entry_width, keep=True)
     return (*outs, entry_weights[None], exit_weights[None])
 
 

time: 154 us -> 152 us (0.987)
  blocking collectives: 118 us -> 105 us
  starting transfers between devices: 13.8 us -> 21.4 us
  other arithmetic: 0 us -> 2.04 us
  waiting for transfers between devices: 6.23 us -> 7.86 us
    all_to_all x1 -> x0, blocking collectives: 13.1 us -> none  [body(): squares = lax.all_to_all(lanes, 'shard', 0, 0)]
    all_to_all x0 -> x1, starting transfers between devices: none -> 7.58 us  [body(): squares = lax.all_to_all(lanes, 'shard', 0, 0)]
    all_to_all x0 -> x1, waiting for transfers between devices: none -> 5.52 us  [body(): squares = lax.all_to_all(lanes, 'shard', 0, 0)]
    ppermute x4, waiting for transfers between devices: 6.23 us -> 2.34 us  [moved(): lax.ppermute(values, 'group', [(i, (i + by) % groups) for i in range(grou...]
    select_n x0 -> x2, other arithmetic: none -> 2.02 us  [placed(): out = jnp.where(here, nearby[turn].reshape(far, 1, own, cols), out)]
  transfers between devices with their start and end apart: 4 -> 5, of which waited for: 2 -> 2; matrix products, arithmetic and copies ran while one was open for 0% -> 1% of each run, Pallas kernels for 0% -> 1%
where the time goes in v4:
time: 152 us; the launch traced here: 150 us
  blocking collectives  105 us (69%)
  starting transfers between devices  21.4 us (14%)
  waiting for transfers between devices  7.86 us (5%)
  Pallas kernels  6.57 us (4%)
  local copies, waits for them, and re-layouts  5.95 us (4%)
  other arithmetic  2.04 us (1%)
    psum x1, blocking collectives, body(): summed = lax.psum(pieces, 'group')  84.1 us
    all_gather x1, blocking collectives, share(): lax.all_gather(rounded, 'group', axis=0, tiled=True, axis_index_groups=st...  21 us
    ppermute x4, starting transfers between devices, moved(): lax.ppermute(values, 'group', [(i, (i + by) % groups) for i in range(grou...  13.8 us
    all_to_all x1, starting transfers between devices, body(): squares = lax.all_to_all(lanes, 'shard', 0, 0)  7.58 us
    all_to_all x1, waiting for transfers between devices, body(): squares = lax.all_to_all(lanes, 'shard', 0, 0)  5.52 us
    pallas_call x2, Pallas kernels, update(): pl.pallas_call(lambda *refs: update_kernel(limit, entry_width, keep, refs...  4.06 us
    slice x6, local copies, waits for them, and re-layouts, pieces_of(): grads[r:r + TILE, c:c + width]  3.92 us
  transfers between devices with their start and end apart: 5, of which 2 were waited for; matrix products, arithmetic and copies ran while one was open for 1% of the time, Pallas kernels for 1%

profile of v4, /device:TPU:6, one launch (start us, length us, event | category | flops | bytes accessed | tf_op | source)
XLA Modules:
  0.0 149.8 jit_solution(13164777960538600695)
XLA Ops:
  0.6 1.0 fusion
  1.7 1.0 fusion.1
  2.7 1.0 fusion.2
  3.8 0.8 fusion.3
  4.6 84.1 %all-reduce.2 = (f32[8,640]{1,0:T(8,128)}, f32[8,640]{1,0:T(8,128)}, f32[8,640]{1,0:T(8,128)}, f32[8,640]{1,0:T(8,128)}, f32[8,640]{1,0:T(8,128)}, /*index=5*/f3...) all-reduce(f32[8,640]{1,0:T(8,128)S(1)} %get-tuple-element.185, ...), channel_id=1, replica_groups=mesh['group'=16,'shard'=32] {'group'}, use_global_device_ids=true, to_apply=%region_0.0 | all-reduce | flops 589824 | bytes 4718592 | tf_op jit(solution)/shard_map/psum | solution.py:170
  88.7 2.5 %own_and_squares.1 = (f32[16,2304]{1,0:T(8,128)}, f32[32,1,128]{2,1,0:T(1,128)}) custom-call(s32[1,1]{1,0:T(1,128)} %bitcast.refs_0_, f32[8,640]{1,0:T(8,128)} %get-tuple-element.26.refs_1_, f32[8,640]{1,0:T(8,128)} %get-tuple-element.27.refs_2_, f32[8,640]{1,0:T(8,128)} %get-tuple-element.28.refs_3_, f32[8,640]{1,0:T(8,128)} %get-tuple-element.29.refs_4_, ...), custom_call_target="tpu_custom_call" | custom-call | tf_op jit(solution)/shard_map/own_and_squares/pallas_call | solution.py:61
  91.2 7.6 %all-to-all-start = ((f32[32,1,128]{2,1,0:T(1,128)}), f32[32,1,128]{2,1,0:T(1,128)S(1)}, u32[]{:S(2)}, u32[]{:S(2)}) async-start(f32[32,1,128]{2,1,0:T(1,128)} %get-tuple-element.17), calls=%async_computation | async-start | bytes 32768 | tf_op jit(solution)/shard_map/all_to_all | solution.py:172
  98.8 5.5 %all-to-all-done.refs_0_ = f32[32,1,128]{2,1,0:T(1,128)S(1)} async-done(((f32[32,1,128]{2,1,0:T(1,128)}), f32[32,1,128]{2,1,0:T(1,128)S(1)}, u32[]{:S(2)}, u32[]{:S(2)}) %all-to-all-start) | async-done | bytes 16416 | tf_op jit(solution)/shard_map/all_to_all | solution.py:172
  104.3 0.6 copy-done.3
  104.9 2.0 %own_weights.1 = bf16[16,2304]{1,0:T(8,128)(2,1)} custom-call(f32[32,1,128]{2,1,0:T(1,128)} %copy-done.3, f32[16,2304]{1,0:T(8,128)} %get-tuple-element.18.refs_1_, f32[1,16,1280]{2,1,0:T(8,128)} %refs_2_.3, f32[1,16,1024]{2,1,0:T(8,128)} %refs_3_.3, f32[1,16,1280]{2,1,0:T(8,128)} %refs_4_.3, f32[1,16,1024]{2,1,0:T(8,128)} %refs_5_.3, ...), custom_call_target="tpu_custom_call" | custom-call | tf_op jit(solution)/shard_map/own_weights/pallas_call | solution.py:115
  107.0 21.0 %all_gather.3 = bf16[64,2304]{1,0:T(8,128)(2,1)S(1)} all-gather(bf16[16,2304]{1,0:T(8,128)(2,1)} %own_weights.1), channel_id=1, replica_groups={{0,128,256,384},{32,160,288,416},{64,192,320,448},{96,224,352,480},{1,1..., dimensions={0}, use_global_device_ids=true | all-gather | bytes 368640 | tf_op jit(solution)/shard_map/all_gather | solution.py:127
  127.9 1.9 %collective-permute-start = (bf16[64,2304]{1,0:T(8,128)(2,1)S(1)}, bf16[64,2304]{1,0:T(8,128)(2,1)S(1)}, u32[]{:S(2)}, u32[]{:S(2)}) collective-permute-start(bf16[64,2304]{1,0:T(8,128)(2,1)S(1)} %all_gather.3), channel_id=1, source_target_pairs={{0,32},{32,64},{64,96},{96,128},{128,160},{160,192},{192,224},{224... | collective-permute-start | bytes 884744 | tf_op jit(solution)/shard_map/ppermute | solution.py:130
  129.9 5.1 %collective-permute-start.2 = (bf16[64,2304]{1,0:T(8,128)(2,1)S(1)}, bf16[64,2304]{1,0:T(8,128)(2,1)S(1)}, u32[]{:S(2)}, u32[]{:S(2)}) collective-permute-start(bf16[64,2304]{1,0:T(8,128)(2,1)S(1)} %all_gather.3), channel_id=1, source_target_pairs={{0,480},{32,0},{64,32},{96,64},{128,96},{160,128},{192,160},{224,1... | collective-permute-start | bytes 884744 | tf_op jit(solution)/shard_map/ppermute | solution.py:130
  135.0 1.9 %collective-permute-start.3 = (bf16[64,1024]{1,0:T(8,128)(2,1)S(1)}, bf16[64,1024]{1,0:T(8,128)(2,1)S(1)}, u32[]{:S(2)}, u32[]{:S(2)}) collective-permute-start(bf16[64,1024]{1,0:T(8,128)(2,1)S(1)} %slice.606), channel_id=1, source_target_pairs={{0,448},{32,480},{64,0},{96,32},{128,64},{160,96},{192,128},{224,1... | collective-permute-start | bytes 393224 | tf_op jit(solution)/shard_map/ppermute | solution.py:130
  137.0 0.1 iota.36
  137.2 0.1 iota.40
  137.3 0.1 iota.43
  137.4 0.1 iota.44
  137.5 4.8 %collective-permute-start.1 = (bf16[64,1280]{1,0:T(8,128)(2,1)S(1)}, bf16[64,1280]{1,0:T(8,128)(2,1)S(1)}, u32[]{:S(2)}, u32[]{:S(2)}) collective-permute-start(bf16[64,1280]{1,0:T(8,128)(2,1)S(1)} %slice.603), channel_id=1, source_target_pairs={{0,64},{32,96},{64,128},{96,160},{128,192},{160,224},{192,256},{22... | collective-permute-start | bytes 491528 | tf_op jit(solution)/shard_map/ppermute | solution.py:130
  142.3 2.1 %own_state.1 = (f32[1,16,1280]{2,1,0:T(8,128)}, f32[1,16,1024]{2,1,0:T(8,128)}, f32[1,16,1280]{2,1,0:T(8,128)}, f32[1,16,1024]{2,1,0:T(8,128)}, f32[1,16,1280]{2,1,0:T(8,128)}, /*index=5*/f32[1,16,1024]{2,1,0:T(8,128)}) custom-call(f32[32,1,128]{2,1,0:T(1,128)} %copy-done.3, f32[16,2304]{1,0:T(8,128)} %get-tuple-element.18.refs_1_, f32[1,16,1280]{2,1,0:T(8,128)} %refs_2_.3, ...), custom_call_target="tpu_custom_call" | custom-call | tf_op jit(solution)/shard_map/own_state/pallas_call | solution.py:115
  144.7 0.4 copy-done.1
  145.2 1.0 select_select_fusion.1
  146.2 2.3 %collective-permute-done.1 = bf16[64,1280]{1,0:T(8,128)(2,1)S(1)} collective-permute-done((bf16[64,1280]{1,0:T(8,128)(2,1)S(1)}, bf16[64,1280]{1,0:T(8,128)(2,1)S(1)}, u32[]{:S(2)}, u32[]{:S(2)}) %collective-permute-start.1) | collective-permute-done | bytes 163872 | tf_op jit(solution)/shard_map/ppermute | solution.py:130
  148.7 1.0 select_select_fusion
  (32 shorter events, 0.7 us)
Async XLA Ops:
  0.6 3.0 %copy-start = (f32[1,1,256,1024]{3,2,1,0:T(8,128)S(1)}, f32[1,1,256,1024]{3,2,1,0:T(8,128)}, u32[]{:S(2)}) copy-start(f32[1,1,256,1024]{3,2,1,0:T(8,128)} %param.9) | copy-start | bytes 3145732
  91.2 13.1 %all-to-all-start = ((f32[32,1,128]{2,1,0:T(1,128)}), f32[32,1,128]{2,1,0:T(1,128)S(1)}, u32[]{:S(2)}, u32[]{:S(2)}) async-start(f32[32,1,128]{2,1,0:T(1,128)} %get-tuple-element.17), calls=%async_computation | async-start | bytes 32768 | tf_op jit(solution)/shard_map/all_to_all | solution.py:172
  104.3 0.6 copy-start.3
  127.9 16.4 %collective-permute-start = (bf16[64,2304]{1,0:T(8,128)(2,1)S(1)}, bf16[64,2304]{1,0:T(8,128)(2,1)S(1)}, u32[]{:S(2)}, u32[]{:S(2)}) collective-permute-start(bf16[64,2304]{1,0:T(8,128)(2,1)S(1)} %all_gather.3), channel_id=1, source_target_pairs={{0,32},{32,64},{64,96},{96,128},{128,160},{160,192},{192,224},{224... | collective-permute-start | bytes 884744 | tf_op jit(solution)/shard_map/ppermute | solution.py:130
  129.9 14.6 %collective-permute-start.2 = (bf16[64,2304]{1,0:T(8,128)(2,1)S(1)}, bf16[64,2304]{1,0:T(8,128)(2,1)S(1)}, u32[]{:S(2)}, u32[]{:S(2)}) collective-permute-start(bf16[64,2304]{1,0:T(8,128)(2,1)S(1)} %all_gather.3), channel_id=1, source_target_pairs={{0,480},{32,0},{64,32},{96,64},{128,96},{160,128},{192,160},{224,1... | collective-permute-start | bytes 884744 | tf_op jit(solution)/shard_map/ppermute | solution.py:130
  135.0 9.4 %collective-permute-start.3 = (bf16[64,1024]{1,0:T(8,128)(2,1)S(1)}, bf16[64,1024]{1,0:T(8,128)(2,1)S(1)}, u32[]{:S(2)}, u32[]{:S(2)}) collective-permute-start(bf16[64,1024]{1,0:T(8,128)(2,1)S(1)} %slice.606), channel_id=1, source_target_pairs={{0,448},{32,480},{64,0},{96,32},{128,64},{160,96},{192,128},{224,1... | collective-permute-start | bytes 393224 | tf_op jit(solution)/shard_map/ppermute | solution.py:130
  137.5 11.0 %collective-permute-start.1 = (bf16[64,1280]{1,0:T(8,128)(2,1)S(1)}, bf16[64,1280]{1,0:T(8,128)(2,1)S(1)}, u32[]{:S(2)}, u32[]{:S(2)}) collective-permute-start(bf16[64,1280]{1,0:T(8,128)(2,1)S(1)} %slice.603), channel_id=1, source_target_pairs={{0,64},{32,96},{64,128},{96,160},{128,192},{160,224},{192,256},{22... | collective-permute-start | bytes 491528 | tf_op jit(solution)/shard_map/ppermute | solution.py:130
  144.4 0.7 copy-start.1
  144.4 0.8 copy-start.2
  145.2 3.3 %slice-start = ((bf16[64,2304]{1,0:T(8,128)(2,1)}), bf16[64,1280]{1,0:T(8,128)(2,1)S(1)}, s32[]{:S(2)}) async-start(bf16[64,2304]{1,0:T(8,128)(2,1)} %copy-done.1), calls=%async_computation.1 | async-start | bytes 327680 | tf_op jit(solution)/shard_map/slice | solution.py:147
  145.2 3.4 %slice-start.1 = ((bf16[64,2304]{1,0:T(8,128)(2,1)}), bf16[64,1280]{1,0:T(8,128)(2,1)S(1)}, s32[]{:S(2)}) async-start(bf16[64,2304]{1,0:T(8,128)(2,1)} %copy-done.2), calls=%async_computation.2 | async-start | bytes 327680 | tf_op jit(solution)/shard_map/slice | solution.py:147

commit v5 on v4

--- a/solution.py
+++ b/solution.py
@@ -84,7 +84,7 @@
     return (master, moment, variance)
 
 
-def update_kernel(limit, entry_width, keep, refs):
+def update_kernel(limit, entry_width, refs):
     squares_ref, total_ref = refs[:2]
     states, outs = refs[2:8], refs[8:]
     clip = clip_of(squares_ref, limit)
@@ -100,22 +100,16 @@
                 total_ref[:, there],
                 clip,
             )
-            if keep:
-                for kind, values in enumerate(stepped):
-                    outs[2 * kind + side][0, :, cols] = values
-            else:
-                outs[0][:, there] = stepped[0].astype(outs[0].dtype)
-
-
-def update(squares, total, states, limit, entry_width, keep):
-    if keep:
-        shapes = [jax.ShapeDtypeStruct(s.shape, s.dtype) for s in states]
-    else:
-        shapes = [jax.ShapeDtypeStruct(total.shape, jnp.bfloat16)]
+            for kind, values in enumerate(stepped):
+                outs[2 * kind + side][0, :, cols] = values
+
+
+def update(squares, total, states, limit, entry_width):
+    shapes = [jax.ShapeDtypeStruct(s.shape, s.dtype) for s in states]
     return pl.pallas_call(
-        lambda *refs: update_kernel(limit, entry_width, keep, refs),
+        lambda *refs: update_kernel(limit, entry_width, refs),
         out_shape=shapes,
-        name="own_state" if keep else "own_weights",
+        name="own_state",
     )(squares, total, *states)
 
 
@@ -133,20 +127,22 @@
     across = (moved(gathered[:, :entry_width], 2), moved(gathered[:, entry_width:], -2))
     me = lax.axis_index("group").astype(jnp.uint32)
 
-    def placed(nearby, cols):
+    def placed(start, middle):
+        cols = middle.shape[1]
         shape = (far, NEAR, own, cols)
         residue = lax.broadcasted_iota(jnp.uint32, shape, 1)
-        out = nearby[0].reshape(far, 1, own, cols)
-        for turn in range(1, NEAR):
+
+        def spread(values):
+            return values.reshape(far, 1, own, values.shape[1])
+
+        nearby = (spread(gathered), spread(ahead), None, spread(behind))
+        out = spread(middle)
+        for turn in (0, 1, 3):
             here = residue == ((me + turn) & (NEAR - 1))
-            out = jnp.where(here, nearby[turn].reshape(far, 1, own, cols), out)
+            out = jnp.where(here, nearby[turn][..., start : start + cols], out)
         return out.reshape(groups * own, cols)
 
-    sides = ((slice(0, entry_width), across[0]), (slice(entry_width, width), across[1]))
-    return gathered, [
-        placed((gathered[:, cols], ahead[:, cols], middle, behind[:, cols]), middle.shape[1])
-        for cols, middle in sides
-    ]
+    return gathered, [placed(0, across[0]), placed(entry_width, across[1])]
 
 
 def body(
@@ -172,10 +168,12 @@
     squares = lax.all_to_all(lanes, "shard", 0, 0)
     limit = ((rows * entry_width + rows * exit_width) * shards) ** 0.5
     states = (entry_params, exit_params, entry_mean, exit_mean, entry_square, exit_square)
-    (rounded,) = update(squares, total, states, limit, entry_width, keep=False)
+    packed = [jnp.concatenate([states[k][0], states[k + 1][0]], axis=1) for k in (0, 2, 4)]
+    clip = jnp.minimum(jnp.float32(1.0), limit / (jnp.sqrt(jnp.sum(squares)) + 1e-06))
+    rounded = adamw_step(*packed, total, clip)[0].astype(jnp.bfloat16)
     gathered, (entry_weights, exit_weights) = share(rounded, entry_width)
     squares, gathered = lax.optimization_barrier((squares, gathered))
-    outs = update(squares, total, states, limit, entry_width, keep=True)
+    outs = update(squares, total, states, limit, entry_width)
     return (*outs, entry_weights[None], exit_weights[None])
 
 

time: 152 us -> 151 us (level)
  Pallas kernels: 6.57 us -> 4.73 us
  other arithmetic: 2.04 us -> 3.76 us
    pallas_call x2 -> x1, Pallas kernels: 4.06 us -> 2.05 us  [update(): pl.pallas_call(lambda *refs: update_kernel(limit, entry_width, refs), out...]
where the time goes in v5:
time: 151 us; the launch traced here: 149 us
  blocking collectives  105 us (70%)
  starting transfers between devices  21.4 us (14%)
  waiting for transfers between devices  7.63 us (5%)
  local copies, waits for them, and re-layouts  4.92 us (3%)
  Pallas kernels  4.73 us (3%)
  other arithmetic  3.76 us (2%)
  between operations  1.71 us (1%)
    psum x1, blocking collectives, body(): summed = lax.psum(pieces, 'group')  84.1 us
    all_gather x1, blocking collectives, share(): lax.all_gather(rounded, 'group', axis=0, tiled=True, axis_index_groups=st...  20.8 us
    ppermute x4, starting transfers between devices, moved(): lax.ppermute(values, 'group', [(i, (i + by) % groups) for i in range(grou...  13.8 us
    all_to_all x1, starting transfers between devices, body(): squares = lax.all_to_all(lanes, 'shard', 0, 0)  7.58 us
    all_to_all x1, waiting for transfers between devices, body(): squares = lax.all_to_all(lanes, 'shard', 0, 0)  4.98 us
    slice x6, local copies, waits for them, and re-layouts, pieces_of(): grads[r:r + TILE, c:c + width]  3.92 us
  transfers between devices with their start and end apart: 5, of which 2 were waited for; matrix products, arithmetic and copies ran while one was open for 1% of the time, Pallas kernels for 1%

profile of v5, /device:TPU:6, one launch (start us, length us, event | category | flops | bytes accessed | tf_op | source)
XLA Modules:
  0.0 149.1 jit_solution(18433364880971530241)
XLA Ops:
  0.6 1.0 fusion.8
  1.7 1.0 fusion.9
  2.7 1.0 fusion.10
  3.8 0.8 fusion.11
  4.6 84.1 %all-reduce.2 = (f32[8,640]{1,0:T(8,128)}, f32[8,640]{1,0:T(8,128)}, f32[8,640]{1,0:T(8,128)}, f32[8,640]{1,0:T(8,128)}, f32[8,640]{1,0:T(8,128)}, /*index=5*/f3...) all-reduce(f32[8,640]{1,0:T(8,128)S(1)} %get-tuple-element.185, ...), channel_id=1, replica_groups=mesh['group'=16,'shard'=32] {'group'}, use_global_device_ids=true, to_apply=%region_0.0 | all-reduce | flops 589824 | bytes 4718592 | tf_op jit(solution)/shard_map/psum | solution.py:166
  88.8 2.7 %own_and_squares.1 = (f32[16,2304]{1,0:T(8,128)}, f32[32,1,128]{2,1,0:T(1,128)}) custom-call(s32[1,1]{1,0:T(1,128)} %bitcast.refs_0_, f32[8,640]{1,0:T(8,128)} %get-tuple-element.26.refs_1_, f32[8,640]{1,0:T(8,128)} %get-tuple-element.27.refs_2_, f32[8,640]{1,0:T(8,128)} %get-tuple-element.28.refs_3_, f32[8,640]{1,0:T(8,128)} %get-tuple-element.29.refs_4_, ...), custom_call_target="tpu_custom_call" | custom-call | tf_op jit(solution)/shard_map/own_and_squares/pallas_call | solution.py:61
  91.4 7.6 %all-to-all-start = ((f32[32,1,128]{2,1,0:T(1,128)}), f32[32,1,128]{2,1,0:T(1,128)S(1)}, u32[]{:S(2)}, u32[]{:S(2)}) async-start(f32[32,1,128]{2,1,0:T(1,128)} %get-tuple-element.17), calls=%async_computation | async-start | bytes 32768 | tf_op jit(solution)/shard_map/all_to_all | solution.py:168
  99.1 0.1 iota.35
  99.2 0.1 iota.36
  99.2 0.1 iota.39
  99.3 0.1 iota.40
  99.5 0.1 iota.44
  99.6 5.0 %all-to-all-done.refs_0_ = f32[32,1,128]{2,1,0:T(1,128)S(1)} async-done(((f32[32,1,128]{2,1,0:T(1,128)}), f32[32,1,128]{2,1,0:T(1,128)S(1)}, u32[]{:S(2)}, u32[]{:S(2)}) %all-to-all-start) | async-done | bytes 16416 | tf_op jit(solution)/shard_map/all_to_all | solution.py:168
  104.6 0.6 reduce_sum.9
  106.0 1.0 subtract_convert_fusion
  107.0 20.8 %all_gather.3 = bf16[64,2304]{1,0:T(8,128)(2,1)S(1)} all-gather(bf16[16,2304]{1,0:T(8,128)(2,1)S(1)} %subtract_convert_fusion), channel_id=1, replica_groups={{0,128,256,384},{32,160,288,416},{64,192,320,448},{96,224,352,480},{1,1..., dimensions={0}, use_global_device_ids=true | all-gather | bytes 368640 | tf_op jit(solution)/shard_map/all_gather | solution.py:121
  127.9 1.9 %collective-permute-start = (bf16[64,2304]{1,0:T(8,128)(2,1)S(1)}, bf16[64,2304]{1,0:T(8,128)(2,1)S(1)}, u32[]{:S(2)}, u32[]{:S(2)}) collective-permute-start(bf16[64,2304]{1,0:T(8,128)(2,1)S(1)} %all_gather.3), channel_id=1, source_target_pairs={{0,32},{32,64},{64,96},{96,128},{128,160},{160,192},{192,224},{224... | collective-permute-start | bytes 884744 | tf_op jit(solution)/shard_map/ppermute | solution.py:124
  129.8 5.1 %collective-permute-start.1 = (bf16[64,2304]{1,0:T(8,128)(2,1)S(1)}, bf16[64,2304]{1,0:T(8,128)(2,1)S(1)}, u32[]{:S(2)}, u32[]{:S(2)}) collective-permute-start(bf16[64,2304]{1,0:T(8,128)(2,1)S(1)} %all_gather.3), channel_id=1, source_target_pairs={{0,480},{32,0},{64,32},{96,64},{128,96},{160,128},{192,160},{224,1... | collective-permute-start | bytes 884744 | tf_op jit(solution)/shard_map/ppermute | solution.py:124
  135.0 1.9 %collective-permute-start.3 = (bf16[64,1024]{1,0:T(8,128)(2,1)S(1)}, bf16[64,1024]{1,0:T(8,128)(2,1)S(1)}, u32[]{:S(2)}, u32[]{:S(2)}) collective-permute-start(bf16[64,1024]{1,0:T(8,128)(2,1)S(1)} %slice.615), channel_id=1, source_target_pairs={{0,448},{32,480},{64,0},{96,32},{128,64},{160,96},{192,128},{224,1... | collective-permute-start | bytes 393224 | tf_op jit(solution)/shard_map/ppermute | solution.py:124
  136.9 4.8 %collective-permute-start.2 = (bf16[64,1280]{1,0:T(8,128)(2,1)S(1)}, bf16[64,1280]{1,0:T(8,128)(2,1)S(1)}, u32[]{:S(2)}, u32[]{:S(2)}) collective-permute-start(bf16[64,1280]{1,0:T(8,128)(2,1)S(1)} %slice.611), channel_id=1, source_target_pairs={{0,64},{32,96},{64,128},{96,160},{128,192},{160,224},{192,256},{22... | collective-permute-start | bytes 491528 | tf_op jit(solution)/shard_map/ppermute | solution.py:124
  141.8 2.1 %own_state.1 = (f32[1,16,1280]{2,1,0:T(8,128)}, f32[1,16,1024]{2,1,0:T(8,128)}, f32[1,16,1280]{2,1,0:T(8,128)}, f32[1,16,1024]{2,1,0:T(8,128)}, f32[1,16,1280]{2,1,0:T(8,128)}, /*index=5*/f32[1,16,1024]{2,1,0:T(8,128)}) custom-call(f32[32,1,128]{2,1,0:T(1,128)} %copy-done.7, f32[16,2304]{1,0:T(8,128)} %get-tuple-element.18.refs_1_, f32[1,16,1280]{2,1,0:T(8,128)} %refs_2_.1, ...), custom_call_target="tpu_custom_call" | custom-call | tf_op jit(solution)/shard_map/own_state/pallas_call | solution.py:109
  144.2 1.0 select_select_fusion.1
  145.2 2.6 %collective-permute-done.2 = bf16[64,1280]{1,0:T(8,128)(2,1)S(1)} collective-permute-done((bf16[64,1280]{1,0:T(8,128)(2,1)S(1)}, bf16[64,1280]{1,0:T(8,128)(2,1)S(1)}, u32[]{:S(2)}, u32[]{:S(2)}) %collective-permute-start.2) | collective-permute-done | bytes 163872 | tf_op jit(solution)/shard_map/ppermute | solution.py:124
  148.0 1.1 select_select_fusion
  (41 shorter events, 0.7 us)
Async XLA Ops:
  0.6 3.0 %copy-start = (f32[1,1,256,1024]{3,2,1,0:T(8,128)S(1)}, f32[1,1,256,1024]{3,2,1,0:T(8,128)}, u32[]{:S(2)}) copy-start(f32[1,1,256,1024]{3,2,1,0:T(8,128)} %param.9) | copy-start | bytes 3145732
  88.7 17.2 %copy-start.1 = (f32[1,16,1280]{2,1,0:T(8,128)S(1)}, f32[1,16,1280]{2,1,0:T(8,128)}, u32[]{:S(2)}) copy-start(f32[1,16,1280]{2,1,0:T(8,128)} %refs_2_.1) | copy-start | bytes 245764
  88.7 17.2 %copy-start.2 = (f32[1,16,1280]{2,1,0:T(8,128)S(1)}, f32[1,16,1280]{2,1,0:T(8,128)}, u32[]{:S(2)}) copy-start(f32[1,16,1280]{2,1,0:T(8,128)} %refs_4_.1) | copy-start | bytes 245764
  88.7 17.2 %copy-start.3 = (f32[1,16,1280]{2,1,0:T(8,128)S(1)}, f32[1,16,1280]{2,1,0:T(8,128)}, u32[]{:S(2)}) copy-start(f32[1,16,1280]{2,1,0:T(8,128)} %refs_6_.1) | copy-start | bytes 245764
  88.7 17.2 %copy-start.4 = (f32[1,16,1024]{2,1,0:T(8,128)S(1)}, f32[1,16,1024]{2,1,0:T(8,128)}, u32[]{:S(2)}) copy-start(f32[1,16,1024]{2,1,0:T(8,128)} %refs_3_.1) | copy-start | bytes 196612
  88.8 17.2 %copy-start.5 = (f32[1,16,1024]{2,1,0:T(8,128)S(1)}, f32[1,16,1024]{2,1,0:T(8,128)}, u32[]{:S(2)}) copy-start(f32[1,16,1024]{2,1,0:T(8,128)} %refs_5_.1) | copy-start | bytes 196612
  88.8 17.2 %copy-start.6 = (f32[1,16,1024]{2,1,0:T(8,128)S(1)}, f32[1,16,1024]{2,1,0:T(8,128)}, u32[]{:S(2)}) copy-start(f32[1,16,1024]{2,1,0:T(8,128)} %refs_7_.1) | copy-start | bytes 196612
  91.4 13.1 %all-to-all-start = ((f32[32,1,128]{2,1,0:T(1,128)}), f32[32,1,128]{2,1,0:T(1,128)S(1)}, u32[]{:S(2)}, u32[]{:S(2)}) async-start(f32[32,1,128]{2,1,0:T(1,128)} %get-tuple-element.17), calls=%async_computation | async-start | bytes 32768 | tf_op jit(solution)/shard_map/all_to_all | solution.py:168
  104.6 37.2 %copy-start.7 = (f32[32,1,128]{2,1,0:T(1,128)}, f32[32,1,128]{2,1,0:T(1,128)S(1)}, u32[]{:S(2)}) copy-start(f32[32,1,128]{2,1,0:T(1,128)S(1)} %all-to-all-done.refs_0_) | copy-start | bytes 49156
  127.9 16.0 %collective-permute-start = (bf16[64,2304]{1,0:T(8,128)(2,1)S(1)}, bf16[64,2304]{1,0:T(8,128)(2,1)S(1)}, u32[]{:S(2)}, u32[]{:S(2)}) collective-permute-start(bf16[64,2304]{1,0:T(8,128)(2,1)S(1)} %all_gather.3), channel_id=1, source_target_pairs={{0,32},{32,64},{64,96},{96,128},{128,160},{160,192},{192,224},{224... | collective-permute-start | bytes 884744 | tf_op jit(solution)/shard_map/ppermute | solution.py:124
  129.8 14.1 %collective-permute-start.1 = (bf16[64,2304]{1,0:T(8,128)(2,1)S(1)}, bf16[64,2304]{1,0:T(8,128)(2,1)S(1)}, u32[]{:S(2)}, u32[]{:S(2)}) collective-permute-start(bf16[64,2304]{1,0:T(8,128)(2,1)S(1)} %all_gather.3), channel_id=1, source_target_pairs={{0,480},{32,0},{64,32},{96,64},{128,96},{160,128},{192,160},{224,1... | collective-permute-start | bytes 884744 | tf_op jit(solution)/shard_map/ppermute | solution.py:124
  135.0 9.0 %collective-permute-start.3 = (bf16[64,1024]{1,0:T(8,128)(2,1)S(1)}, bf16[64,1024]{1,0:T(8,128)(2,1)S(1)}, u32[]{:S(2)}, u32[]{:S(2)}) collective-permute-start(bf16[64,1024]{1,0:T(8,128)(2,1)S(1)} %slice.615), channel_id=1, source_target_pairs={{0,448},{32,480},{64,0},{96,32},{128,64},{160,96},{192,128},{224,1... | collective-permute-start | bytes 393224 | tf_op jit(solution)/shard_map/ppermute | solution.py:124
  136.9 10.9 %collective-permute-start.2 = (bf16[64,1280]{1,0:T(8,128)(2,1)S(1)}, bf16[64,1280]{1,0:T(8,128)(2,1)S(1)}, u32[]{:S(2)}, u32[]{:S(2)}) collective-permute-start(bf16[64,1280]{1,0:T(8,128)(2,1)S(1)} %slice.611), channel_id=1, source_target_pairs={{0,64},{32,96},{64,128},{96,160},{128,192},{160,224},{192,256},{22... | collective-permute-start | bytes 491528 | tf_op jit(solution)/shard_map/ppermute | solution.py:124

commit v6 on v5

--- a/solution.py
+++ b/solution.py
@@ -15,22 +15,19 @@
 
 LANES = 128
 TILE = 8
-ENTRY_PIECE = 640
-EXIT_PIECE = 1024
 NEAR = 4
 
 
-def pieces_of(grads, width):
-    rows, cols = grads.shape
-    return [
-        grads[r : r + TILE, c : c + width]
-        for r in range(0, rows, TILE)
-        for c in range(0, cols, width)
-    ]
-
-
-def places_of(rows, cols, width, start):
-    return [(r, start + c) for r in range(0, rows, TILE) for c in range(0, cols, width)]
+def cuts_of(rows, width, splits):
+    cuts = []
+    for top in range(0, rows, TILE):
+        wide = width // 2 if top < splits * TILE else width
+        cuts += [(top, col, wide) for col in range(0, width, wide)]
+    return cuts
+
+
+def pieces_of(grads, cuts):
+    return [grads[r : r + TILE, c : c + wide] for r, c, wide in cuts]
 
 
 def own_and_squares_kernel(places, own, me_ref, *refs):
@@ -159,10 +156,11 @@
     exit_width = exit_grads.shape[3]
     own = entry_params.shape[1]
     shards = lax.axis_size("shard")
-    pieces = pieces_of(entry_grads.reshape(rows, entry_width), ENTRY_PIECE)
-    pieces += pieces_of(exit_grads.reshape(rows, exit_width), EXIT_PIECE)
-    places = places_of(rows, entry_width, ENTRY_PIECE, 0)
-    places += places_of(rows, exit_width, EXIT_PIECE, entry_width)
+    entry_cuts, exit_cuts = cuts_of(rows, entry_width, 0), cuts_of(rows, exit_width, 1)
+    entry_local = entry_grads.reshape(rows, entry_width)
+    exit_pieces = pieces_of(exit_grads.reshape(rows, exit_width), exit_cuts)
+    pieces = pieces_of(entry_local, entry_cuts) + exit_pieces
+    places = [(r, c) for r, c, _ in entry_cuts] + [(r, entry_width + c) for r, c, _ in exit_cuts]
     summed = lax.psum(pieces, "group")
     total, lanes = own_and_squares(summed, places, own, entry_width + exit_width, shards)
     squares = lax.all_to_all(lanes, "shard", 0, 0)

time: 151 us -> 151 us (level)
  waiting for transfers between devices: 7.63 us -> 10.2 us
  blocking collectives: 105 us -> 103 us
  local copies, waits for them, and re-layouts: 4.92 us -> 3.39 us
    ppermute x4, waiting for transfers between devices: 2.65 us -> 5.18 us  [moved(): lax.ppermute(values, 'group', [(i, (i + by) % groups) for i in range(grou...]
    slice x6 -> x5, local copies, waits for them, and re-layouts: 3.92 us -> 2.39 us  [pieces_of(): return [grads[r:r + TILE, c:c + wide] for r, c, wide in cuts]]
  transfers between devices with their start and end apart: 5 -> 5, of which waited for: 2 -> 3; matrix products, arithmetic and copies ran while one was open for 1% -> 1% of each run, Pallas kernels for 1% -> 1%
where the time goes in v6:
time: 151 us; the launch traced here: 148 us
  blocking collectives  103 us (68%)
  starting transfers between devices  21.4 us (14%)
  waiting for transfers between devices  10.2 us (7%)
  Pallas kernels  4.74 us (3%)
  other arithmetic  3.76 us (2%)
  local copies, waits for them, and re-layouts  3.39 us (2%)
  between operations  1.71 us (1%)
    psum x1, blocking collectives, body(): summed = lax.psum(pieces, 'group')  82.9 us
    all_gather x1, blocking collectives, share(): lax.all_gather(rounded, 'group', axis=0, tiled=True, axis_index_groups=st...  20.5 us
    ppermute x4, starting transfers between devices, moved(): lax.ppermute(values, 'group', [(i, (i + by) % groups) for i in range(grou...  13.8 us
    all_to_all x1, starting transfers between devices, body(): squares = lax.all_to_all(lanes, 'shard', 0, 0)  7.58 us
    ppermute x4, waiting for transfers between devices, moved(): lax.ppermute(values, 'group', [(i, (i + by) % groups) for i in range(grou...  5.18 us
    all_to_all x1, waiting for transfers between devices, body(): squares = lax.all_to_all(lanes, 'shard', 0, 0)  4.98 us
  transfers between devices with their start and end apart: 5, of which 3 were waited for; matrix products, arithmetic and copies ran while one was open for 1% of the time, Pallas kernels for 1%

profile of v6, /device:TPU:6, one launch (start us, length us, event | category | flops | bytes accessed | tf_op | source)
XLA Modules:
  0.0 148.5 jit_solution(5007176276979607456)
XLA Ops:
  0.6 1.2 slice_bitcast_fusion.6
  1.9 1.1 slice_bitcast_fusion.7
  3.1 82.9 %all-reduce.2 = (f32[8,1280]{1,0:T(8,128)}, f32[8,1280]{1,0:T(8,128)}, f32[8,1280]{1,0:T(8,128)}, f32[8,1280]{1,0:T(8,128)}, f32[8,1280]{1,0:T(8,128)}, /*index=...) all-reduce(f32[8,1280]{1,0:T(8,128)S(1)} %get-tuple-element.122, ...), channel_id=1, replica_groups=mesh['group'=16,'shard'=32] {'group'}, use_global_device_ids=true, to_apply=%region_0.0 | all-reduce | flops 589824 | bytes 4718592 | tf_op jit(solution)/shard_map/psum | solution.py:164
  86.0 2.7 %own_and_squares.1 = (f32[16,2304]{1,0:T(8,128)}, f32[32,1,128]{2,1,0:T(1,128)}) custom-call(s32[1,1]{1,0:T(1,128)} %bitcast.refs_0_, f32[8,1280]{1,0:T(8,128)} %get-tuple-element.26.refs_1_, f32[8,1280]{1,0:T(8,128)} %get-tuple-element.27.refs_2_, f32[8,1280]{1,0:T(8,128)} %get-tuple-element.28.refs_3_, f32[8,1280]{1,0:T(8,128)} %get-tuple-element.29.refs_4_, ...), custom_call_target="tpu_custom_call" | custom-call | tf_op jit(solution)/shard_map/own_and_squares/pallas_call | solution.py:58
  88.6 7.6 %all-to-all-start = ((f32[32,1,128]{2,1,0:T(1,128)}), f32[32,1,128]{2,1,0:T(1,128)S(1)}, u32[]{:S(2)}, u32[]{:S(2)}) async-start(f32[32,1,128]{2,1,0:T(1,128)} %get-tuple-element.17), calls=%async_computation | async-start | bytes 32768 | tf_op jit(solution)/shard_map/all_to_all | solution.py:166
  96.3 0.1 iota.35
  96.4 0.1 iota.36
  96.4 0.1 iota.39
  96.5 0.1 iota.40
  96.6 0.1 iota.43
  96.7 0.1 iota.44
  96.8 5.0 %all-to-all-done.refs_0_ = f32[32,1,128]{2,1,0:T(1,128)S(1)} async-done(((f32[32,1,128]{2,1,0:T(1,128)}), f32[32,1,128]{2,1,0:T(1,128)S(1)}, u32[]{:S(2)}, u32[]{:S(2)}) %all-to-all-start) | async-done | bytes 16416 | tf_op jit(solution)/shard_map/all_to_all | solution.py:166
  101.8 0.6 reduce_sum.9
  103.2 1.0 subtract_convert_fusion
  104.2 20.5 %all_gather.3 = bf16[64,2304]{1,0:T(8,128)(2,1)S(1)} all-gather(bf16[16,2304]{1,0:T(8,128)(2,1)S(1)} %subtract_convert_fusion), channel_id=1, replica_groups={{0,128,256,384},{32,160,288,416},{64,192,320,448},{96,224,352,480},{1,1..., dimensions={0}, use_global_device_ids=true | all-gather | bytes 368640 | tf_op jit(solution)/shard_map/all_gather | solution.py:118
  124.7 1.9 %collective-permute-start = (bf16[64,2304]{1,0:T(8,128)(2,1)S(1)}, bf16[64,2304]{1,0:T(8,128)(2,1)S(1)}, u32[]{:S(2)}, u32[]{:S(2)}) collective-permute-start(bf16[64,2304]{1,0:T(8,128)(2,1)S(1)} %all_gather.3), channel_id=1, source_target_pairs={{0,32},{32,64},{64,96},{96,128},{128,160},{160,192},{192,224},{224... | collective-permute-start | bytes 884744 | tf_op jit(solution)/shard_map/ppermute | solution.py:121
  126.6 5.1 %collective-permute-start.1 = (bf16[64,2304]{1,0:T(8,128)(2,1)S(1)}, bf16[64,2304]{1,0:T(8,128)(2,1)S(1)}, u32[]{:S(2)}, u32[]{:S(2)}) collective-permute-start(bf16[64,2304]{1,0:T(8,128)(2,1)S(1)} %all_gather.3), channel_id=1, source_target_pairs={{0,480},{32,0},{64,32},{96,64},{128,96},{160,128},{192,160},{224,1... | collective-permute-start | bytes 884744 | tf_op jit(solution)/shard_map/ppermute | solution.py:121
  131.8 2.5 %collective-permute-start.3 = (bf16[64,1024]{1,0:T(8,128)(2,1)S(1)}, bf16[64,1024]{1,0:T(8,128)(2,1)S(1)}, u32[]{:S(2)}, u32[]{:S(2)}) collective-permute-start(bf16[64,1024]{1,0:T(8,128)(2,1)S(1)} %slice.553), channel_id=1, source_target_pairs={{0,448},{32,480},{64,0},{96,32},{128,64},{160,96},{192,128},{224,1... | collective-permute-start | bytes 393224 | tf_op jit(solution)/shard_map/ppermute | solution.py:121
  134.3 4.2 %collective-permute-start.2 = (bf16[64,1280]{1,0:T(8,128)(2,1)S(1)}, bf16[64,1280]{1,0:T(8,128)(2,1)S(1)}, u32[]{:S(2)}, u32[]{:S(2)}) collective-permute-start(bf16[64,1280]{1,0:T(8,128)(2,1)S(1)} %slice.549), channel_id=1, source_target_pairs={{0,64},{32,96},{64,128},{96,160},{128,192},{160,224},{192,256},{22... | collective-permute-start | bytes 491528 | tf_op jit(solution)/shard_map/ppermute | solution.py:121
  138.6 2.1 %own_state.1 = (f32[1,16,1280]{2,1,0:T(8,128)}, f32[1,16,1024]{2,1,0:T(8,128)}, f32[1,16,1280]{2,1,0:T(8,128)}, f32[1,16,1024]{2,1,0:T(8,128)}, f32[1,16,1280]{2,1,0:T(8,128)}, /*index=5*/f32[1,16,1024]{2,1,0:T(8,128)}) custom-call(f32[32,1,128]{2,1,0:T(1,128)} %copy-done.7, f32[16,2304]{1,0:T(8,128)} %get-tuple-element.18.refs_1_, f32[1,16,1280]{2,1,0:T(8,128)} %refs_2_.1, ...), custom_call_target="tpu_custom_call" | custom-call | tf_op jit(solution)/shard_map/own_state/pallas_call | solution.py:106
  140.8 0.5 collective-permute-done.3
  141.5 1.0 select_select_fusion.1
  142.5 4.7 %collective-permute-done.2 = bf16[64,1280]{1,0:T(8,128)(2,1)S(1)} collective-permute-done((bf16[64,1280]{1,0:T(8,128)(2,1)S(1)}, bf16[64,1280]{1,0:T(8,128)(2,1)S(1)}, u32[]{:S(2)}, u32[]{:S(2)}) %collective-permute-start.2) | collective-permute-done | bytes 163872 | tf_op jit(solution)/shard_map/ppermute | solution.py:121
  147.4 1.1 select_select_fusion
  (40 shorter events, 0.6 us)
Async XLA Ops:
  0.6 2.3 %copy-start = (f32[1,1,256,1024]{3,2,1,0:T(8,128)S(1)}, f32[1,1,256,1024]{3,2,1,0:T(8,128)}, u32[]{:S(2)}) copy-start(f32[1,1,256,1024]{3,2,1,0:T(8,128)} %param.9) | copy-start | bytes 3145732
  85.9 17.2 %copy-start.1 = (f32[1,16,1280]{2,1,0:T(8,128)S(1)}, f32[1,16,1280]{2,1,0:T(8,128)}, u32[]{:S(2)}) copy-start(f32[1,16,1280]{2,1,0:T(8,128)} %refs_2_.1) | copy-start | bytes 245764
  85.9 17.2 %copy-start.2 = (f32[1,16,1280]{2,1,0:T(8,128)S(1)}, f32[1,16,1280]{2,1,0:T(8,128)}, u32[]{:S(2)}) copy-start(f32[1,16,1280]{2,1,0:T(8,128)} %refs_4_.1) | copy-start | bytes 245764
  85.9 17.2 %copy-start.3 = (f32[1,16,1280]{2,1,0:T(8,128)S(1)}, f32[1,16,1280]{2,1,0:T(8,128)}, u32[]{:S(2)}) copy-start(f32[1,16,1280]{2,1,0:T(8,128)} %refs_6_.1) | copy-start | bytes 245764
  85.9 17.2 %copy-start.4 = (f32[1,16,1024]{2,1,0:T(8,128)S(1)}, f32[1,16,1024]{2,1,0:T(8,128)}, u32[]{:S(2)}) copy-start(f32[1,16,1024]{2,1,0:T(8,128)} %refs_3_.1) | copy-start | bytes 196612
  85.9 17.2 %copy-start.5 = (f32[1,16,1024]{2,1,0:T(8,128)S(1)}, f32[1,16,1024]{2,1,0:T(8,128)}, u32[]{:S(2)}) copy-start(f32[1,16,1024]{2,1,0:T(8,128)} %refs_5_.1) | copy-start | bytes 196612
  86.0 17.2 %copy-start.6 = (f32[1,16,1024]{2,1,0:T(8,128)S(1)}, f32[1,16,1024]{2,1,0:T(8,128)}, u32[]{:S(2)}) copy-start(f32[1,16,1024]{2,1,0:T(8,128)} %refs_7_.1) | copy-start | bytes 196612
  88.6 13.1 %all-to-all-start = ((f32[32,1,128]{2,1,0:T(1,128)}), f32[32,1,128]{2,1,0:T(1,128)S(1)}, u32[]{:S(2)}, u32[]{:S(2)}) async-start(f32[32,1,128]{2,1,0:T(1,128)} %get-tuple-element.17), calls=%async_computation | async-start | bytes 32768 | tf_op jit(solution)/shard_map/all_to_all | solution.py:166
  101.8 36.8 %copy-start.7 = (f32[32,1,128]{2,1,0:T(1,128)}, f32[32,1,128]{2,1,0:T(1,128)S(1)}, u32[]{:S(2)}) copy-start(f32[32,1,128]{2,1,0:T(1,128)S(1)} %all-to-all-done.refs_0_) | copy-start | bytes 49156
  124.7 16.0 %collective-permute-start = (bf16[64,2304]{1,0:T(8,128)(2,1)S(1)}, bf16[64,2304]{1,0:T(8,128)(2,1)S(1)}, u32[]{:S(2)}, u32[]{:S(2)}) collective-permute-start(bf16[64,2304]{1,0:T(8,128)(2,1)S(1)} %all_gather.3), channel_id=1, source_target_pairs={{0,32},{32,64},{64,96},{96,128},{128,160},{160,192},{192,224},{224... | collective-permute-start | bytes 884744 | tf_op jit(solution)/shard_map/ppermute | solution.py:121
  126.6 14.1 %collective-permute-start.1 = (bf16[64,2304]{1,0:T(8,128)(2,1)S(1)}, bf16[64,2304]{1,0:T(8,128)(2,1)S(1)}, u32[]{:S(2)}, u32[]{:S(2)}) collective-permute-start(bf16[64,2304]{1,0:T(8,128)(2,1)S(1)} %all_gather.3), channel_id=1, source_target_pairs={{0,480},{32,0},{64,32},{96,64},{128,96},{160,128},{192,160},{224,1... | collective-permute-start | bytes 884744 | tf_op jit(solution)/shard_map/ppermute | solution.py:121
  131.8 9.5 %collective-permute-start.3 = (bf16[64,1024]{1,0:T(8,128)(2,1)S(1)}, bf16[64,1024]{1,0:T(8,128)(2,1)S(1)}, u32[]{:S(2)}, u32[]{:S(2)}) collective-permute-start(bf16[64,1024]{1,0:T(8,128)(2,1)S(1)} %slice.553), channel_id=1, source_target_pairs={{0,448},{32,480},{64,0},{96,32},{128,64},{160,96},{192,128},{224,1... | collective-permute-start | bytes 393224 | tf_op jit(solution)/shard_map/ppermute | solution.py:121
  134.3 12.9 %collective-permute-start.2 = (bf16[64,1280]{1,0:T(8,128)(2,1)S(1)}, bf16[64,1280]{1,0:T(8,128)(2,1)S(1)}, u32[]{:S(2)}, u32[]{:S(2)}) collective-permute-start(bf16[64,1280]{1,0:T(8,128)(2,1)S(1)} %slice.549), channel_id=1, source_target_pairs={{0,64},{32,96},{64,128},{96,160},{128,192},{160,224},{192,256},{22... | collective-permute-start | bytes 491528 | tf_op jit(solution)/shard_map/ppermute | solution.py:121

commit v7 on v6

--- a/solution.py
+++ b/solution.py
@@ -121,25 +121,25 @@
         return lax.ppermute(values, "group", [(i, (i + by) % groups) for i in range(groups)])
 
     ahead, behind = moved(gathered, -1), moved(gathered, 1)
-    across = (moved(gathered[:, :entry_width], 2), moved(gathered[:, entry_width:], -2))
+    cut = entry_width // 2
+    left, right = moved(gathered[:, :cut], 2), moved(gathered[:, cut:], -2)
+    across = (jnp.concatenate([left, right[:, :cut]], axis=1), right[:, cut:])
     me = lax.axis_index("group").astype(jnp.uint32)
 
-    def placed(start, middle):
-        cols = middle.shape[1]
+    def placed(nearby, cols):
         shape = (far, NEAR, own, cols)
         residue = lax.broadcasted_iota(jnp.uint32, shape, 1)
-
-        def spread(values):
-            return values.reshape(far, 1, own, values.shape[1])
-
-        nearby = (spread(gathered), spread(ahead), None, spread(behind))
-        out = spread(middle)
-        for turn in (0, 1, 3):
+        out = nearby[0].reshape(far, 1, own, cols)
+        for turn in range(1, NEAR):
             here = residue == ((me + turn) & (NEAR - 1))
-            out = jnp.where(here, nearby[turn][..., start : start + cols], out)
+            out = jnp.where(here, nearby[turn].reshape(far, 1, own, cols), out)
         return out.reshape(groups * own, cols)
 
-    return gathered, [placed(0, across[0]), placed(entry_width, across[1])]
+    sides = ((slice(0, entry_width), across[0]), (slice(entry_width, width), across[1]))
+    return gathered, [
+        placed((gathered[:, cols], ahead[:, cols], middle, behind[:, cols]), middle.shape[1])
+        for cols, middle in sides
+    ]
 
 
 def body(

time: 151 us -> 150 us (level)
  transfers between devices with their start and end apart: 5 -> 5, of which waited for: 3 -> 2; matrix products, arithmetic and copies ran while one was open for 1% -> 0% of each run, Pallas kernels for 1% -> 1%
where the time goes in v7:
time: 150 us; the launch traced here: 148 us
  blocking collectives  103 us (69%)
  starting transfers between devices  20.3 us (14%)
  waiting for transfers between devices  10.3 us (7%)
  Pallas kernels  4.74 us (3%)
  local copies, waits for them, and re-layouts  4.22 us (3%)
  other arithmetic  3.74 us (2%)
  between operations  1.74 us (1%)
    psum x1, blocking collectives, body(): summed = lax.psum(pieces, 'group')  82.9 us
    all_gather x1, blocking collectives, share(): lax.all_gather(rounded, 'group', axis=0, tiled=True, axis_index_groups=st...  20.5 us
    ppermute x4, starting transfers between devices, moved(): lax.ppermute(values, 'group', [(i, (i + by) % groups) for i in range(grou...  12.7 us
    all_to_all x1, starting transfers between devices, body(): squares = lax.all_to_all(lanes, 'shard', 0, 0)  7.58 us
    all_to_all x1, waiting for transfers between devices, body(): squares = lax.all_to_all(lanes, 'shard', 0, 0)  5.34 us
    ppermute x4, waiting for transfers between devices, moved(): lax.ppermute(values, 'group', [(i, (i + by) % groups) for i in range(grou...  4.98 us
  transfers between devices with their start and end apart: 5, of which 2 were waited for; matrix products, arithmetic and copies ran while one was open for 0% of the time, Pallas kernels for 1%

profile of v7, /device:TPU:6, one launch (start us, length us, event | category | flops | bytes accessed | tf_op | source)
XLA Modules:
  0.0 148.4 jit_solution(11116798839979359771)
XLA Ops:
  0.6 1.2 slice_bitcast_fusion
  1.9 1.1 slice_bitcast_fusion.1
  3.1 82.9 %all-reduce.2 = (f32[8,1280]{1,0:T(8,128)}, f32[8,1280]{1,0:T(8,128)}, f32[8,1280]{1,0:T(8,128)}, f32[8,1280]{1,0:T(8,128)}, f32[8,1280]{1,0:T(8,128)}, /*index=...) all-reduce(f32[8,1280]{1,0:T(8,128)S(1)} %get-tuple-element.122, ...), channel_id=1, replica_groups=mesh['group'=16,'shard'=32] {'group'}, use_global_device_ids=true, to_apply=%region_0.0 | all-reduce | flops 589824 | bytes 4718592 | tf_op jit(solution)/shard_map/psum | solution.py:164
  86.0 2.7 %own_and_squares.1 = (f32[16,2304]{1,0:T(8,128)}, f32[32,1,128]{2,1,0:T(1,128)}) custom-call(s32[1,1]{1,0:T(1,128)} %bitcast.refs_0_, f32[8,1280]{1,0:T(8,128)} %get-tuple-element.26.refs_1_, f32[8,1280]{1,0:T(8,128)} %get-tuple-element.27.refs_2_, f32[8,1280]{1,0:T(8,128)} %get-tuple-element.28.refs_3_, f32[8,1280]{1,0:T(8,128)} %get-tuple-element.29.refs_4_, ...), custom_call_target="tpu_custom_call" | custom-call | tf_op jit(solution)/shard_map/own_and_squares/pallas_call | solution.py:58
  88.6 7.6 %all-to-all-start = ((f32[32,1,128]{2,1,0:T(1,128)}), f32[32,1,128]{2,1,0:T(1,128)S(1)}, u32[]{:S(2)}, u32[]{:S(2)}) async-start(f32[32,1,128]{2,1,0:T(1,128)} %get-tuple-element.17), calls=%async_computation | async-start | bytes 32768 | tf_op jit(solution)/shard_map/all_to_all | solution.py:166
  96.2 0.1 iota.35
  96.3 0.1 iota.36
  96.4 5.3 %all-to-all-done.refs_0_ = f32[32,1,128]{2,1,0:T(1,128)S(1)} async-done(((f32[32,1,128]{2,1,0:T(1,128)}), f32[32,1,128]{2,1,0:T(1,128)S(1)}, u32[]{:S(2)}, u32[]{:S(2)}) %all-to-all-start) | async-done | bytes 16416 | tf_op jit(solution)/shard_map/all_to_all | solution.py:166
  101.8 0.6 reduce_sum.9
  103.2 1.0 subtract_convert_fusion
  104.2 20.5 %all_gather.3 = bf16[64,2304]{1,0:T(8,128)(2,1)S(1)} all-gather(bf16[16,2304]{1,0:T(8,128)(2,1)S(1)} %subtract_convert_fusion), channel_id=1, replica_groups={{0,128,256,384},{32,160,288,416},{64,192,320,448},{96,224,352,480},{1,1..., dimensions={0}, use_global_device_ids=true | all-gather | bytes 368640 | tf_op jit(solution)/shard_map/all_gather | solution.py:118
  124.7 3.8 %collective-permute-start.2 = (bf16[64,1664]{1,0:T(8,128)(2,1)S(1)}, bf16[64,1664]{1,0:T(8,128)(2,1)S(1)}, u32[]{:S(2)}, u32[]{:S(2)}) collective-permute-start(bf16[64,1664]{1,0:T(8,128)(2,1)S(1)} %slice.556), channel_id=1, source_target_pairs={{0,448},{32,480},{64,0},{96,32},{128,64},{160,96},{192,128},{224,1... | collective-permute-start | bytes 638984 | tf_op jit(solution)/shard_map/ppermute | solution.py:121
  128.5 0.1 iota.39
  128.6 0.1 iota.40
  128.7 2.2 %collective-permute-start = (bf16[64,2304]{1,0:T(8,128)(2,1)S(1)}, bf16[64,2304]{1,0:T(8,128)(2,1)S(1)}, u32[]{:S(2)}, u32[]{:S(2)}) collective-permute-start(bf16[64,2304]{1,0:T(8,128)(2,1)S(1)} %all_gather.3), channel_id=1, source_target_pairs={{0,32},{32,64},{64,96},{96,128},{128,160},{160,192},{192,224},{224... | collective-permute-start | bytes 884744 | tf_op jit(solution)/shard_map/ppermute | solution.py:121
  130.9 4.8 %collective-permute-start.3 = (bf16[64,2304]{1,0:T(8,128)(2,1)S(1)}, bf16[64,2304]{1,0:T(8,128)(2,1)S(1)}, u32[]{:S(2)}, u32[]{:S(2)}) collective-permute-start(bf16[64,2304]{1,0:T(8,128)(2,1)S(1)} %all_gather.3), channel_id=1, source_target_pairs={{0,480},{32,0},{64,32},{96,64},{128,96},{160,128},{192,160},{224,1... | collective-permute-start | bytes 884744 | tf_op jit(solution)/shard_map/ppermute | solution.py:121
  135.8 1.9 %collective-permute-start.1 = (bf16[64,640]{1,0:T(8,128)(2,1)S(1)}, bf16[64,640]{1,0:T(8,128)(2,1)S(1)}, u32[]{:S(2)}, u32[]{:S(2)}) collective-permute-start(bf16[64,640]{1,0:T(8,128)(2,1)S(1)} %slice.555), channel_id=1, source_target_pairs={{0,64},{32,96},{64,128},{96,160},{128,192},{160,224},{192,256},{22... | collective-permute-start | bytes 245768 | tf_op jit(solution)/shard_map/ppermute | solution.py:121
  137.7 0.1 iota.43
  137.8 0.1 iota.44
  137.9 2.1 %own_state.1 = (f32[1,16,1280]{2,1,0:T(8,128)}, f32[1,16,1024]{2,1,0:T(8,128)}, f32[1,16,1280]{2,1,0:T(8,128)}, f32[1,16,1024]{2,1,0:T(8,128)}, f32[1,16,1280]{2,1,0:T(8,128)}, /*index=5*/f32[1,16,1024]{2,1,0:T(8,128)}) custom-call(f32[32,1,128]{2,1,0:T(1,128)} %copy-done.8, f32[16,2304]{1,0:T(8,128)} %get-tuple-element.18.refs_1_, f32[1,16,1280]{2,1,0:T(8,128)} %refs_2_.1, ...), custom_call_target="tpu_custom_call" | custom-call | tf_op jit(solution)/shard_map/own_state/pallas_call | solution.py:106
  140.0 5.0 %collective-permute-done.1 = bf16[64,640]{1,0:T(8,128)(2,1)S(1)} collective-permute-done((bf16[64,640]{1,0:T(8,128)(2,1)S(1)}, bf16[64,640]{1,0:T(8,128)(2,1)S(1)}, u32[]{:S(2)}, u32[]{:S(2)}) %collective-permute-start.1) | collective-permute-done | bytes 81952 | tf_op jit(solution)/shard_map/ppermute | solution.py:121
  145.3 1.0 select_select_fusion.1
  146.4 0.8 slice-done
  147.3 1.0 select_select_fusion
  (46 shorter events, 0.7 us)
Async XLA Ops:
  0.6 2.3 %copy-start = (f32[1,1,256,1024]{3,2,1,0:T(8,128)S(1)}, f32[1,1,256,1024]{3,2,1,0:T(8,128)}, u32[]{:S(2)}) copy-start(f32[1,1,256,1024]{3,2,1,0:T(8,128)} %param.9) | copy-start | bytes 3145732
  85.9 17.2 %copy-start.2 = (f32[1,16,1280]{2,1,0:T(8,128)S(1)}, f32[1,16,1280]{2,1,0:T(8,128)}, u32[]{:S(2)}) copy-start(f32[1,16,1280]{2,1,0:T(8,128)} %refs_2_.1) | copy-start | bytes 245764
  85.9 17.2 %copy-start.3 = (f32[1,16,1280]{2,1,0:T(8,128)S(1)}, f32[1,16,1280]{2,1,0:T(8,128)}, u32[]{:S(2)}) copy-start(f32[1,16,1280]{2,1,0:T(8,128)} %refs_4_.1) | copy-start | bytes 245764
  85.9 17.2 %copy-start.4 = (f32[1,16,1280]{2,1,0:T(8,128)S(1)}, f32[1,16,1280]{2,1,0:T(8,128)}, u32[]{:S(2)}) copy-start(f32[1,16,1280]{2,1,0:T(8,128)} %refs_6_.1) | copy-start | bytes 245764
  85.9 17.2 %copy-start.5 = (f32[1,16,1024]{2,1,0:T(8,128)S(1)}, f32[1,16,1024]{2,1,0:T(8,128)}, u32[]{:S(2)}) copy-start(f32[1,16,1024]{2,1,0:T(8,128)} %refs_3_.1) | copy-start | bytes 196612
  85.9 17.2 %copy-start.6 = (f32[1,16,1024]{2,1,0:T(8,128)S(1)}, f32[1,16,1024]{2,1,0:T(8,128)}, u32[]{:S(2)}) copy-start(f32[1,16,1024]{2,1,0:T(8,128)} %refs_5_.1) | copy-start | bytes 196612
  86.0 17.2 %copy-start.7 = (f32[1,16,1024]{2,1,0:T(8,128)S(1)}, f32[1,16,1024]{2,1,0:T(8,128)}, u32[]{:S(2)}) copy-start(f32[1,16,1024]{2,1,0:T(8,128)} %refs_7_.1) | copy-start | bytes 196612
  88.6 13.1 %all-to-all-start = ((f32[32,1,128]{2,1,0:T(1,128)}), f32[32,1,128]{2,1,0:T(1,128)S(1)}, u32[]{:S(2)}, u32[]{:S(2)}) async-start(f32[32,1,128]{2,1,0:T(1,128)} %get-tuple-element.17), calls=%async_computation | async-start | bytes 32768 | tf_op jit(solution)/shard_map/all_to_all | solution.py:166
  101.8 36.2 %copy-start.8 = (f32[32,1,128]{2,1,0:T(1,128)}, f32[32,1,128]{2,1,0:T(1,128)S(1)}, u32[]{:S(2)}) copy-start(f32[32,1,128]{2,1,0:T(1,128)S(1)} %all-to-all-done.refs_0_) | copy-start | bytes 49156
  124.7 15.3 %collective-permute-start.2 = (bf16[64,1664]{1,0:T(8,128)(2,1)S(1)}, bf16[64,1664]{1,0:T(8,128)(2,1)S(1)}, u32[]{:S(2)}, u32[]{:S(2)}) collective-permute-start(bf16[64,1664]{1,0:T(8,128)(2,1)S(1)} %slice.556), channel_id=1, source_target_pairs={{0,448},{32,480},{64,0},{96,32},{128,64},{160,96},{192,128},{224,1... | collective-permute-start | bytes 638984 | tf_op jit(solution)/shard_map/ppermute | solution.py:121
  128.7 16.3 %collective-permute-start = (bf16[64,2304]{1,0:T(8,128)(2,1)S(1)}, bf16[64,2304]{1,0:T(8,128)(2,1)S(1)}, u32[]{:S(2)}, u32[]{:S(2)}) collective-permute-start(bf16[64,2304]{1,0:T(8,128)(2,1)S(1)} %all_gather.3), channel_id=1, source_target_pairs={{0,32},{32,64},{64,96},{96,128},{128,160},{160,192},{192,224},{224... | collective-permute-start | bytes 884744 | tf_op jit(solution)/shard_map/ppermute | solution.py:121
  130.9 14.1 %collective-permute-start.3 = (bf16[64,2304]{1,0:T(8,128)(2,1)S(1)}, bf16[64,2304]{1,0:T(8,128)(2,1)S(1)}, u32[]{:S(2)}, u32[]{:S(2)}) collective-permute-start(bf16[64,2304]{1,0:T(8,128)(2,1)S(1)} %all_gather.3), channel_id=1, source_target_pairs={{0,480},{32,0},{64,32},{96,64},{128,96},{160,128},{192,160},{224,1... | collective-permute-start | bytes 884744 | tf_op jit(solution)/shard_map/ppermute | solution.py:121
  135.8 9.2 %collective-permute-start.1 = (bf16[64,640]{1,0:T(8,128)(2,1)S(1)}, bf16[64,640]{1,0:T(8,128)(2,1)S(1)}, u32[]{:S(2)}, u32[]{:S(2)}) collective-permute-start(bf16[64,640]{1,0:T(8,128)(2,1)S(1)} %slice.555), channel_id=1, source_target_pairs={{0,64},{32,96},{64,128},{96,160},{128,192},{160,224},{192,256},{22... | collective-permute-start | bytes 245768 | tf_op jit(solution)/shard_map/ppermute | solution.py:121
  145.0 1.3 copy-start.1
  146.3 0.9 slice-start
